TPU v7x, 32 devices: a whole 2x2x4 slice. The times are simulated.
32 devices in a mesh: vocab: 16 (over z, y, core), tok: 2 (over x).
Axes of the slice: x: 2, y: 2, z: 4, core: 2. Of those that a mesh axis runs over, the one named last changes fastest.
Arguments:
- hidden: bfloat16 [256, 3584], P('tok', 'vocab'), may hold values from -8 to 8
- head_weight: bfloat16 [3584, 81920], P('tok', 'vocab'), may hold values from -4 to 4
- targets: int32 [256], P('tok'), may hold values from 0 to 81919
- response_mask: int32 [256], P('tok'), may hold values 0 or 1
- labels: int32 [2], P('tok'), may hold values 0 or 1
- reference_sums: float32 [2, 2], P('tok'), may hold values from -48 to 48
Outputs:
- mean_loss: float32 [], replicated
- margins: float32 [2], P('tok')
- hidden_grad: bfloat16 [256, 3584], P('tok', 'vocab')
- head_grad: bfloat16 [3584, 81920], P('tok', 'vocab')
All inputs are finite; a program needn't handle non-finite values. No bound on the sum of `response_mask` or of `labels` on one device may be relied on, other than what follows from the above.
Results may differ from a plain program's by a relative error of at most 0.0085.
Values may be sent and summed in bfloat16 or wider, within the bound.
No kernel may reach another device: no remote copies, remote signals or barrier semaphores. Data moves between devices by JAX's collectives and lax.ppermute only.
A program may use at most 128 MiB of HBM per device.

v0:
```python
import math

import jax
import jax.numpy as jnp
from jax import lax
from jax.sharding import PartitionSpec as P

beta_scale = 0.1
tie_offset = math.log(2.0)
tie_const = math.log(3.0)
grad_scale = 512.0


def pair_terms(margins, labels):
    winner = labels.astype(jnp.float32)
    log_tie = (
        tie_const
        + margins
        - tie_offset
        - jax.nn.softplus(margins - tie_offset)
        - jax.nn.softplus(margins + tie_offset)
    )
    losses = winner * jax.nn.softplus(tie_offset - margins) - (1.0 - winner) * log_tie
    slopes = -winner * jax.nn.sigmoid(tie_offset - margins) - (1.0 - winner) * (
        1.0 - jax.nn.sigmoid(margins - tie_offset) - jax.nn.sigmoid(margins + tie_offset)
    )
    return (losses, slopes)


def add_parts(received):
    return jnp.sum(received, axis=0)


def local(hidden, head_weight, targets, response_mask, labels, reference_sums):
    tok_rows = hidden.shape[0]
    vocab_cols = head_weight.shape[1]
    tok_count = lax.axis_size("tok")
    pair_local = labels.shape[0]
    pair_total = pair_local * tok_count
    span = tok_rows // (2 * pair_local)
    rows_full = lax.all_gather(hidden, "vocab", axis=1, tiled=True)
    token_cols = lax.all_to_all(rows_full, "tok", split_axis=1, concat_axis=0, tiled=True)
    partial_value = jnp.dot(token_cols, head_weight, preferred_element_type=jnp.float32)
    partial_value = partial_value.reshape(tok_count, tok_rows, vocab_cols)
    logits = add_parts(
        lax.all_to_all(partial_value, "tok", split_axis=0, concat_axis=0, tiled=True)
    )
    offset = lax.axis_index("vocab") * vocab_cols
    columns = lax.broadcasted_iota(jnp.int32, (1, vocab_cols), 1) + offset
    matched = columns == targets[:, None]
    local_max = jnp.max(logits, axis=1)
    local_target = jnp.sum(jnp.where(matched, logits, 0.0), axis=1)
    row_max = lax.pmax(local_max, "vocab")
    shifted = jnp.exp(logits - row_max[:, None])
    totals, target_logit = lax.psum((jnp.sum(shifted, axis=1), local_target), "vocab")
    probs = shifted / totals[:, None]
    token_logp = target_logit - (row_max + jnp.log(totals))
    weights = response_mask.astype(jnp.float32)
    sequence_logp = jnp.sum((token_logp * weights).reshape(pair_local, 2, span), axis=2)
    ratios = sequence_logp - reference_sums
    margins = beta_scale * (ratios[:, 0] - ratios[:, 1])
    losses, slopes = pair_terms(margins, labels)
    mean_loss = lax.psum(jnp.sum(losses), "tok") / pair_total
    pair_coef = beta_scale * grad_scale / pair_total * slopes
    signed = jnp.stack([pair_coef, -pair_coef], axis=1)
    token_coef = (
        jnp.broadcast_to(signed[:, :, None], (pair_local, 2, span)).reshape(tok_rows) * weights
    )
    onehot = jnp.where(matched, 1.0, 0.0).astype(jnp.float32)
    dlogits = (token_coef[:, None] * (onehot - probs)).astype(jnp.bfloat16)
    dlogit_all = lax.all_gather(dlogits, "tok", axis=0, tiled=True)
    head_grad = lax.dot_general(
        token_cols, dlogit_all, (((0,), (0,)), ((), ())), preferred_element_type=jnp.float32
    ).astype(jnp.bfloat16)
    partial_grad = lax.dot_general(
        head_weight, dlogit_all, (((1,), (1,)), ((), ())), preferred_element_type=jnp.float32
    )
    returned = lax.all_to_all(
        partial_grad.astype(jnp.bfloat16), "tok", split_axis=1, concat_axis=0, tiled=True
    ).astype(partial_grad.dtype)
    grad_cols = lax.psum_scatter(returned, "vocab", scatter_dimension=0, tiled=True)
    hidden_grad = grad_cols.T.astype(jnp.bfloat16)
    return (mean_loss, margins, hidden_grad, head_grad)


def solution(mesh):
    return jax.shard_map(
        local,
        mesh=mesh,
        in_specs=(
            P("tok", "vocab"),
            P("tok", "vocab"),
            P("tok"),
            P("tok"),
            P("tok"),
            P("tok", None),
        ),
        out_specs=(P(), P("tok"), P("tok", "vocab"), P("tok", "vocab")),
        check_vma=False,
    )
```

profile of v0, /device:TPU:0, one launch (start us, length us, event | category | flops | bytes accessed | tf_op | source)
XLA Modules:
  0.0 336.2 jit_solution(5547884590679001420)
XLA Ops:
  7.2 26.1 %all_gather.6 = bf16[128,3584]{0,1:T(8,128)(2,1)S(1)} all-gather(bf16[128,224]{0,1:T(8,128)(2,1)} %param.6), channel_id=1, replica_groups=mesh['vocab'=16,'tok'=2] {'vocab'}, dimensions={1}, use_global_device_ids=true | all-gather | bytes 974848 | tf_op jit(solution)/shard_map/all_gather | solution.py:41
  33.8 15.4 %all_to_all.37 = bf16[128,2,1792]{2,0,1:T(8,128)(2,1)S(1)} all-to-all(bf16[128,2,1792]{2,0,1:T(8,128)(2,1)S(1)} %copy.15), channel_id=1, replica_groups=mesh['vocab'=16,'tok'=2] {'tok'}, dimensions={1} | all-to-all | bytes 1835008 | tf_op jit(solution)/shard_map/all_to_all | solution.py:42
  49.3 12.8 %fusion = f32[2,128,5120]{2,1,0:T(8,128)} fusion(bf16[1792,5120]{1,0:T(8,128)(2,1)} %param.7, bf16[128,2,1792]{2,0,1:T(8,128)(2,1)S(1)} %all_to_all.37), kind=kOutput, calls=%fused_computation.1 | convolution fusion | flops 4697620480 | bytes 24510464 | tf_op jit(solution)/shard_map/dot_general | solution.py:43
  62.1 6.0 %all-to-all-start.1 = ((f32[2,128,5120]{2,1,0:T(8,128)}), f32[2,128,5120]{2,1,0:T(8,128)}, u32[]{:S(2)}, u32[]{:S(2)}) async-start(f32[2,128,5120]{2,1,0:T(8,128)} %fusion), calls=%async_computation.1 | async-start | bytes 10485760 | tf_op jit(solution)/shard_map/all_to_all | solution.py:46
  69.3 57.1 %all-to-all-done.1 = f32[2,128,5120]{2,1,0:T(8,128)} async-done(((f32[2,128,5120]{2,1,0:T(8,128)}), f32[2,128,5120]{2,1,0:T(8,128)}, u32[]{:S(2)}, u32[]{:S(2)}) %all-to-all-start.1) | async-done | bytes 5242912 | tf_op jit(solution)/shard_map/all_to_all | solution.py:46
  126.5 3.1 reduce_sum.44
  129.8 29.5 %pmax.7 = f32[128]{0:T(128)S(1)} all-reduce(f32[128]{0:T(128)S(1)} %reduce_max.9), channel_id=1, replica_groups=mesh['vocab'=16,'tok'=2] {'vocab'}, use_global_device_ids=true, to_apply=%region_4.5 | all-reduce | flops 128 | bytes 1024 | tf_op jit(solution)/shard_map/pmax | solution.py:53
  159.3 2.0 fusion.7
  161.3 30.1 %all-reduce = (f32[128]{0:T(128)}, f32[128]{0:T(128)S(1)}) all-reduce(f32[128]{0:T(128)} %get-tuple-element.17, f32[128]{0:T(128)S(1)} %get-tuple-element.16), channel_id=1, replica_groups=mesh['vocab'=16,'tok'=2] {'vocab'}, use_global_device_ids=true, to_apply=%region_2.3 | all-reduce | flops 256 | bytes 2048 | tf_op jit(solution)/shard_map/psum | solution.py:55
  191.4 1.2 convert_multiply_fusion.1
  192.6 0.7 reshape.41
  193.3 0.6 reduce_sum.47
  194.0 0.7 bitcast_subtract_fusion
  197.5 0.7 convert_multiply_fusion
  198.2 2.7 fusion.6
  200.9 35.2 %all-gather.2.cloned.1.call-done = bf16[256,5120]{1,0:T(8,128)(2,1)} async-done(((bf16[128,5120]{1,0:T(8,128)(2,1)}), bf16[256,5120]{1,0:T(8,128)(2,1)}) %all-gather.2.cloned.1.call-update) | async-done | bytes 2621456 | tf_op jit(solution)/shard_map/all_gather | solution.py:71
  236.1 11.9 %convolution_convert_fusion.1 = bf16[256,1792]{1,0:T(8,128)(2,1)S(1)} fusion(bf16[256,5120]{1,0:T(8,128)(2,1)} %all-gather.2.cloned.1.call-done, bf16[1792,5120]{1,0:T(8,128)(2,1)} %param.7), kind=kOutput, calls=%fused_computation.11 | convolution fusion | flops 4698079232 | bytes 21889024 | tf_op jit(solution)/shard_map/dot_general | solution.py:75
  248.1 14.7 %all_to_all.38 = bf16[1792,2,128]{0,2,1:T(8,128)(2,1)S(1)} all-to-all(bf16[1792,2,128]{0,2,1:T(8,128)(2,1)S(1)} %bitcast.34), channel_id=1, replica_groups=mesh['vocab'=16,'tok'=2] {'tok'}, dimensions={1} | all-to-all | bytes 1835008 | tf_op jit(solution)/shard_map/all_to_all | solution.py:78
  262.9 1.7 copy.16
  265.0 6.2 %psum.23 = f32[]{:T(128)} all-reduce(f32[]{:T(128)} %bitcast.5), channel_id=1, replica_groups=mesh['vocab'=16,'tok'=2] {'tok'}, use_global_device_ids=true, to_apply=%region_8.9 | all-reduce | flops 1 | bytes 8 | tf_op jit(solution)/shard_map/psum | solution.py:63
  271.9 11.4 %fusion.2 = bf16[1792,5120]{0,1:T(8,128)(2,1)} fusion(bf16[256,5120]{1,0:T(8,128)(2,1)} %all-gather.2.cloned.1.call-done, bf16[256,1792]{1,0:T(8,128)(2,1)S(1)} %bitcast.33), kind=kOutput, calls=%fused_computation.3 | convolution fusion | flops 4706795520 | bytes 21889024 | tf_op jit(solution)/shard_map/dot_general | solution.py:72
  283.2 25.0 %copy.17 = bf16[1792,5120]{1,0:T(8,128)(2,1)} copy(bf16[1792,5120]{0,1:T(8,128)(2,1)} %fusion.2) | data formatting | bytes 36700160
  308.2 17.3 %reduce-scatter.2.cloned.1.call-done = f32[224,128]{1,0:T(8,128)} async-done(((f32[3584,128]{1,0:T(8,128)}), f32[224,128]{1,0:T(8,128)}) %reduce-scatter.2.cloned.1.call-update) | async-done | bytes 114704 | tf_op jit(solution)/shard_map/reduce_scatter | solution.py:81
  325.5 1.5 convert_bitcast_fusion.1
  (14 shorter events, 2.9 us)
Async XLA Ops:
  62.1 64.4 %all-to-all-start.1 = ((f32[2,128,5120]{2,1,0:T(8,128)}), f32[2,128,5120]{2,1,0:T(8,128)}, u32[]{:S(2)}, u32[]{:S(2)}) async-start(f32[2,128,5120]{2,1,0:T(8,128)} %fusion), calls=%async_computation.1 | async-start | bytes 10485760 | tf_op jit(solution)/shard_map/all_to_all | solution.py:46
  68.0 168.1 %all-gather.2.cloned.1.call-start = ((), (), s32[]{:S(2)}) async-start(), calls=%async_computation.4 | async-start | bytes 3932160 | tf_op jit(solution)/shard_map/all_gather | solution.py:71
  129.6 29.7 %copy-start = (s32[128]{0:T(128)S(1)}, s32[128]{0:T(128)}, u32[]{:S(2)}) copy-start(s32[128]{0:T(128)} %param.8) | copy-start | bytes 1540
  200.9 124.6 %reduce-scatter.2.cloned.1.call-start = ((), (), s32[]{:S(2)}) async-start(), calls=%async_computation.5 | async-start | bytes 1949696 | tf_op jit(solution)/shard_map/reduce_scatter | solution.py:81
Sparse Core Ops, SparseCore 0:
  201.0 35.0 all-gather.1
  264.8 60.6 reduce-scatter.1
where the time goes:
time: 337 us; the launch traced here: 336 us
  blocking collectives  122 us (36%)
  waiting for transfers between devices  110 us (33%)
  matrix products  36.1 us (11%)
  local copies, waits for them, and re-layouts  29.2 us (9%)
  between operations  19.5 us (6%)
  other arithmetic  13.5 us (4%)
  starting transfers between devices  6.04 us (2%)
    all_to_all x1, waiting for transfers between devices, local(): lax.all_to_all(partial_value, 'tok', split_axis=0, concat_axis=0, tiled=T...  57.1 us
    all_gather x1, waiting for transfers between devices, local(): dlogit_all = lax.all_gather(dlogits, 'tok', axis=0, tiled=True)  35.2 us
    psum x1, blocking collectives, local(): lax.psum((jnp.sum(shifted, axis=1), local_target), 'vocab')  30.1 us
    pmax x1, blocking collectives, local(): row_max = lax.pmax(local_max, 'vocab')  29.5 us
    all_gather x1, blocking collectives, local(): rows_full = lax.all_gather(hidden, 'vocab', axis=1, tiled=True)  26.1 us
    unnamed x3, local copies, waits for them, and re-layouts  25 us
    reduce_scatter x1, waiting for transfers between devices, local(): lax.psum_scatter(returned, 'vocab', scatter_dimension=0, tiled=True)  17.3 us
    all_to_all x1, blocking collectives, local(): lax.all_to_all(rows_full, 'tok', split_axis=1, concat_axis=0, tiled=True)  15.4 us
  transfers between devices with their start and end apart: 3, of which 3 were waited for; matrix products, arithmetic and copies ran while one was open for 11% of the time, Pallas kernels for 0%

commit v1 on v0

--- a/solution.py
+++ b/solution.py
@@ -1,9 +1,13 @@
+import functools
 import math
 
 import jax
 import jax.numpy as jnp
 from jax import lax
+from jax.experimental import pallas as pl
+from jax.experimental.pallas import tpu as pltpu
 from jax.sharding import PartitionSpec as P
+
 
 beta_scale = 0.1
 tie_offset = math.log(2.0)
@@ -31,7 +35,7 @@
     return jnp.sum(received, axis=0)
 
 
-def local(hidden, head_weight, targets, response_mask, labels, reference_sums):
+def general_local(hidden, head_weight, targets, response_mask, labels, reference_sums):
     tok_rows = hidden.shape[0]
     vocab_cols = head_weight.shape[1]
     tok_count = lax.axis_size("tok")
@@ -83,9 +87,669 @@
     return (mean_loss, margins, hidden_grad, head_grad)
 
 
+swap_pairs = ((0, 1), (1, 0))
+hidden_bound = 8.0
+weight_bound = 4.0
+half_limit = 60000.0
+part_tiles = (4, 4, 8, 8, 8, 4, 4)
+mebi = 1 << 20
+
+
+def exclusive(count, mask):
+    return [(spot, spot ^ mask) for spot in range(count)]
+
+
+def across(value, count, mask):
+    return lax.ppermute(value, "vocab", exclusive(count, mask))
+
+
+def over(value):
+    return lax.ppermute(value, "tok", swap_pairs)
+
+
+def plane_swap(value, count, moves):
+    half = count // 2
+    pairs = []
+    for plane in range(2):
+        for spot in range(count):
+            if spot // half != plane:
+                pairs.append((2 * spot + plane, 2 * (spot ^ half) + 1 - plane))
+    received = lax.ppermute(value, ("vocab", "tok"), pairs)
+    return jnp.where(moves, received, value)
+
+
+def place_kernel(order, spot_ref, *refs):
+    hidden_t_ref, hidden_n_ref = refs[-2:]
+    slots, feats, rows = refs[0].shape
+    half = 2 * slots
+    spot = spot_ref[0]
+    for side, ref in zip((0, 2, 1, 3), refs[:-2]):
+        for slot in range(slots):
+            source = spot ^ (order[slot] ^ side)
+            start = pl.multiple_of((source % half) * feats, 32)
+            column = pl.multiple_of((source // half) * rows, 128)
+            hidden_t_ref[pl.ds(start, feats), pl.ds(column, rows)] = ref[slot]
+    depth = hidden_t_ref.shape[0]
+    step = 256 if depth % 256 == 0 else 128
+    for start in range(0, depth, step):
+        hidden_n_ref[:, start : start + step] = hidden_t_ref[start : start + step, :].T
+
+
+def fold_kernel(start, has_state, logits_ref, target_ref, weight_ref, *refs):
+    if has_state:
+        stats_ref, grad_ref, new_stats_ref, new_grad_ref, terms_ref = refs
+    else:
+        new_stats_ref, new_grad_ref, terms_ref = refs
+    logits = logits_ref[...]
+    width = logits.shape[1]
+    columns = lax.broadcasted_iota(jnp.int32, logits.shape, 1) + start
+    hit = columns == target_ref[...]
+    top = jnp.max(logits, axis=1, keepdims=True)
+    if has_state:
+        old = stats_ref[...].T
+        old_top = old[:, 0:1]
+        top = jnp.maximum(top, old_top)
+    terms = jnp.exp(logits - top)
+    total = jnp.sum(terms, axis=1, keepdims=True)
+    target = jnp.sum(jnp.where(hit, logits, 0.0), axis=1, keepdims=True)
+    terms_ref[...] = jnp.where(hit, 0.0, terms).astype(jnp.bfloat16)
+    shrink = jnp.ones_like(top)
+    if has_state:
+        shrink = jnp.exp(old_top - top)
+        total = total + old[:, 1:2] * shrink
+        target = target + old[:, 2:3]
+    lane = lax.broadcasted_iota(jnp.int32, (logits.shape[0], 128), 1)
+    packed = jnp.where(
+        lane == 0, top, jnp.where(lane == 1, total, jnp.where(lane == 2, target, shrink))
+    ).T
+    new_stats_ref[...] = packed[0:8]
+    shrink_row = packed[3:4]
+    depth = weight_ref.shape[0]
+    step = depth // 2 if depth % 256 == 0 else depth
+    for first in range(0, depth, step):
+        part = lax.dot_general(
+            weight_ref[first : first + step, start : start + width],
+            terms_ref[...],
+            (((1,), (1,)), ((), ())),
+            preferred_element_type=jnp.float32,
+        )
+        if has_state:
+            part = part + grad_ref[first : first + step, :] * shrink_row
+        new_grad_ref[first : first + step, :] = part
+
+
+def fold(start, width, logits, local_targets, head_weight, state):
+    tokens = logits.shape[0]
+    depth = head_weight.shape[0]
+    args = [logits, local_targets, head_weight]
+    aliases = {}
+    if state is not None:
+        args += list(state)
+        aliases = {4: 1}
+    return pl.pallas_call(
+        functools.partial(fold_kernel, start, state is not None),
+        out_shape=(
+            jax.ShapeDtypeStruct((8, tokens), jnp.float32),
+            jax.ShapeDtypeStruct((depth, tokens), jnp.float32),
+        ),
+        in_specs=vmem_specs(len(args)),
+        out_specs=tuple(vmem_specs(2)),
+        scratch_shapes=[pltpu.VMEM((tokens, width), jnp.bfloat16)],
+        input_output_aliases=aliases,
+        compiler_params=pltpu.CompilerParams(vmem_limit_bytes=12 * mebi),
+        cost_estimate=pl.CostEstimate(
+            flops=2 * depth * tokens * width,
+            transcendentals=tokens * width,
+            bytes_accessed=2 * depth * width + 4 * tokens * width + 8 * depth * tokens,
+        ),
+    )(*args)
+
+
+def load_kernel(source_ref, held_ref, sems):
+    number = sems.shape[0]
+    rows = source_ref.shape[0] // number
+    copies = [
+        pltpu.make_async_copy(
+            source_ref.at[pl.ds(index * rows, rows)],
+            held_ref.at[pl.ds(index * rows, rows)],
+            sems.at[index],
+        )
+        for index in range(number)
+    ]
+    for copy in copies:
+        copy.start()
+    for copy in copies:
+        copy.wait()
+
+
+def load(head_weight):
+    depth = head_weight.shape[0]
+    number = 8 if depth % 256 == 0 else 1
+    return pl.pallas_call(
+        load_kernel,
+        out_shape=pltpu.VMEM(head_weight.shape, head_weight.dtype),
+        in_specs=[pl.BlockSpec(memory_space=pl.ANY)],
+        out_specs=pl.BlockSpec(memory_space=pltpu.VMEM),
+        scratch_shapes=[pltpu.SemaphoreType.DMA((number,))],
+        compiler_params=pltpu.CompilerParams(vmem_limit_bytes=20 * mebi),
+        cost_estimate=pl.CostEstimate(
+            flops=0, transcendentals=0, bytes_accessed=2 * head_weight.size
+        ),
+    )(head_weight)
+
+
+def logit_kernel(start, hidden_ref, weight_ref, out_ref):
+    width = out_ref.shape[1]
+    step = 256 if width % 256 == 0 else width
+    for first in range(0, width, step):
+        out_ref[:, first : first + step] = jnp.dot(
+            hidden_ref[...],
+            weight_ref[:, start + first : start + first + step],
+            preferred_element_type=jnp.float32,
+        )
+
+
+def logit_part(start, width, hidden_n, head_weight):
+    tokens, depth = hidden_n.shape
+    return pl.pallas_call(
+        functools.partial(logit_kernel, start),
+        out_shape=jax.ShapeDtypeStruct((tokens, width), jnp.float32),
+        in_specs=vmem_specs(2),
+        out_specs=vmem_specs(1)[0],
+        compiler_params=pltpu.CompilerParams(vmem_limit_bytes=12 * mebi),
+        cost_estimate=pl.CostEstimate(
+            flops=2 * depth * tokens * width, transcendentals=0, bytes_accessed=2 * depth * width
+        ),
+    )(hidden_n, head_weight)
+
+
+def gather_hidden(piece, where, count):
+    order = [0]
+    parts = [piece]
+    for mask in range(4, count, 4):
+        order.append(mask)
+        parts.append(across(piece, count, mask))
+    feats, rows = piece.shape
+    stacked = jnp.concatenate(parts, axis=0)
+    side = across(stacked, count, 2)
+    groups = [stacked, side, across(stacked, count, 1), across(side, count, 1)]
+    slots = len(order)
+    depth = 2 * slots * feats
+    return pl.pallas_call(
+        lambda *refs: place_kernel(order, *refs),
+        out_shape=(
+            jax.ShapeDtypeStruct((depth, 2 * rows), piece.dtype),
+            jax.ShapeDtypeStruct((2 * rows, depth), piece.dtype),
+        ),
+        in_specs=[pl.BlockSpec(memory_space=pltpu.SMEM)]
+        + [pl.BlockSpec(memory_space=pltpu.VMEM)] * len(groups),
+        out_specs=[pl.BlockSpec(memory_space=pltpu.VMEM)] * 2,
+        compiler_params=pltpu.CompilerParams(vmem_limit_bytes=8 * mebi),
+        cost_estimate=pl.CostEstimate(flops=0, transcendentals=0, bytes_accessed=4000000),
+    )(
+        where,
+        *[group.reshape(slots, feats, rows) for group in groups],
+    )
+
+
+def pick_kernel(feats, spot_ref, target_ref, weight_ref, keep_ref, send_ref, sum_ref):
+    _, cols = weight_ref.shape
+    width = 1024 if cols % 1024 == 0 else cols
+    columns = lax.broadcasted_iota(jnp.int32, (target_ref.shape[0], width), 1)
+    for start in range(0, cols, width):
+        hit = columns + start == target_ref[...]
+        part = lax.dot_general(
+            weight_ref[:, start : start + width],
+            jnp.where(hit, 1.0, 0.0).astype(jnp.bfloat16),
+            (((1,), (1,)), ((), ())),
+            preferred_element_type=jnp.float32,
+        )
+        if start == 0:
+            sum_ref[...] = part
+        else:
+            sum_ref[...] += part
+    bit = spot_ref[0] % 2
+    for group in range(keep_ref.shape[0] // feats):
+        out = pl.ds(group * feats, feats)
+        near = pl.multiple_of((2 * group + bit) * feats, 8)
+        far = pl.multiple_of((2 * group + 1 - bit) * feats, 8)
+        keep_ref[out, :] = sum_ref[pl.ds(near, feats), :].astype(jnp.bfloat16)
+        send_ref[out, :] = sum_ref[pl.ds(far, feats), :].astype(jnp.bfloat16)
+
+
+def pick_next_kernel(feats, spot_ref, old_ref, got_ref, keep_ref, send_ref):
+    def value(group):
+        rows = pl.ds(pl.multiple_of(group * feats, 16), feats)
+        return old_ref[rows, :] + got_ref[rows, :]
+
+    bit = (spot_ref[0] // 2) % 2
+    for group in range(keep_ref.shape[0] // feats):
+        out = pl.ds(group * feats, feats)
+        keep_ref[out, :] = value(2 * group + bit)
+        send_ref[out, :] = value(2 * group + 1 - bit)
+
+
+def pick_spread_kernel(feats, spot_ref, old_ref, got_ref, *outs):
+    place = spot_ref[0] // 4
+    rows = outs[0].shape[1]
+    for shift in range(4):
+        chosen = place ^ shift
+        group = pl.ds(pl.multiple_of((chosen % 2) * feats, 16), feats)
+        value = old_ref[group, :].astype(jnp.float32) + got_ref[group, :].astype(jnp.float32)
+        value = jnp.where(chosen // 2 == 0, value[:, :rows], value[:, rows:])
+        outs[shift][...] = value.astype(jnp.bfloat16)
+
+
+def pick(where, local_targets, head_weight, count):
+    tokens = local_targets.shape[0]
+    depth, cols = head_weight.shape
+    feats = 2 * depth // count
+    rows = tokens // 2
+    bf16 = jnp.bfloat16
+    keep, send = pl.pallas_call(
+        functools.partial(pick_kernel, feats),
+        out_shape=[jax.ShapeDtypeStruct((depth // 2, tokens), bf16)] * 2,
+        in_specs=[pl.BlockSpec(memory_space=pltpu.SMEM)] + vmem_specs(2),
+        out_specs=vmem_specs(2),
+        scratch_shapes=[pltpu.VMEM((depth, tokens), jnp.float32)],
+        compiler_params=pltpu.CompilerParams(vmem_limit_bytes=14 * mebi),
+        cost_estimate=pl.CostEstimate(
+            flops=2 * depth * tokens * cols,
+            transcendentals=0,
+            bytes_accessed=2 * depth * cols,
+        ),
+    )(where, local_targets, head_weight)
+    got = across(send, count, 1)
+    keep, send = small_call(
+        functools.partial(pick_next_kernel, feats),
+        [((depth // 4, tokens), bf16)] * 2,
+        [where, keep, got],
+    )
+    got = across(send, count, 2)
+    keep, *sends = small_call(
+        functools.partial(pick_spread_kernel, feats),
+        [((feats, rows), bf16)] * 4,
+        [where, keep, got],
+    )
+    return [keep] + [across(send, count, 4 * shift) for shift, send in zip((1, 2, 3), sends)]
+
+
+def side_kernel(cols, place_ref, own_ref, other_ref, rows_ref, target_ref):
+    swap = place_ref[1] != 0
+    own, other = own_ref[...], other_ref[...]
+    both = jnp.concatenate(
+        [jnp.where(swap, other, own), jnp.where(swap, own, other)], axis=1
+    )
+    rows_ref[...] = both
+    target_ref[...] = both.T[:, 0:1].astype(jnp.int32) - place_ref[0] * cols
+
+
+def vmem_specs(number):
+    return [pl.BlockSpec(memory_space=pltpu.VMEM)] * number
+
+
+def split_rows(rows):
+    high = rows.astype(jnp.bfloat16)
+    rest = rows - high.astype(jnp.float32)
+    middle = rest.astype(jnp.bfloat16)
+    low = (rest - middle.astype(jnp.float32)).astype(jnp.bfloat16)
+    return [high, middle, low]
+
+
+def put_stats(ref, start, rows):
+    for index, block in enumerate(split_rows(jnp.concatenate([rows, rows], axis=0))):
+        ref[start + 16 * index : start + 16 * index + 16, :] = block
+
+
+def get_stats(ref, start):
+    blocks = [
+        ref[start + 16 * index : start + 16 * index + 16, :].astype(jnp.float32)[0:8]
+        for index in range(3)
+    ]
+    return blocks[0] + blocks[1] + blocks[2]
+
+
+def merged_rows(bit, own, other):
+    swap = bit != 0
+    first = jnp.where(swap, other, own)
+    second = jnp.where(swap, own, other)
+    top = jnp.maximum(first[0:1], second[0:1])
+    total = first[1:2] * jnp.exp(first[0:1] - top) + second[1:2] * jnp.exp(second[0:1] - top)
+    target = first[2:3] + second[2:3]
+    return jnp.concatenate([top, total, target, jnp.zeros((5, own.shape[1]), own.dtype)], axis=0)
+
+
+def first_half_kernel(feats, spot_ref, grad_ref, stats_ref, keep_ref, send_ref):
+    bit = spot_ref[0] % 2
+    groups = keep_ref.shape[0] // feats
+    for group in range(groups):
+        out = pl.ds(group * feats, feats)
+        near = pl.multiple_of((2 * group + bit) * feats, 8)
+        far = pl.multiple_of((2 * group + 1 - bit) * feats, 8)
+        keep_ref[out, :] = grad_ref[pl.ds(near, feats), :]
+        send_ref[out, :] = grad_ref[pl.ds(far, feats), :].astype(jnp.bfloat16)
+    put_stats(send_ref, groups * feats, stats_ref[...])
+
+
+def halved(old_ref, got_ref, stats_ref, bit):
+    own = stats_ref[...]
+    other = get_stats(got_ref, old_ref.shape[0])
+    merged = merged_rows(bit, own, other)
+    return merged, jnp.exp(own[0:1] - merged[0:1]), jnp.exp(other[0:1] - merged[0:1])
+
+
+def next_half_kernel(
+    feats, mask, spot_ref, old_ref, got_ref, stats_ref, keep_ref, send_ref, new_stats_ref
+):
+    spot = spot_ref[0]
+    merged, own_factor, other_factor = halved(old_ref, got_ref, stats_ref, (spot // mask) % 2)
+
+    def value(group):
+        rows = pl.ds(pl.multiple_of(group * feats, 16), feats)
+        return old_ref[rows, :] * own_factor + got_ref[rows, :].astype(jnp.float32) * other_factor
+
+    bit = (spot // (2 * mask)) % 2
+    groups = keep_ref.shape[0] // feats
+    for group in range(groups):
+        out = pl.ds(group * feats, feats)
+        keep_ref[out, :] = value(2 * group + bit)
+        send_ref[out, :] = value(2 * group + 1 - bit).astype(jnp.bfloat16)
+    put_stats(send_ref, groups * feats, merged)
+    new_stats_ref[...] = merged
+
+
+def spread_kernel(feats, spot_ref, old_ref, got_ref, stats_ref, keep_ref, new_stats_ref, *sends):
+    spot = spot_ref[0]
+    merged, own_factor, other_factor = halved(old_ref, got_ref, stats_ref, (spot // 2) % 2)
+    new_stats_ref[...] = merged
+    place = spot // 4
+    rows = keep_ref.shape[1]
+    for shift in range(4):
+        chosen = place ^ shift
+        group = pl.ds(pl.multiple_of((chosen % 2) * feats, 16), feats)
+        left = chosen // 2 == 0
+        value = old_ref[group, :] * own_factor + got_ref[group, :].astype(jnp.float32) * other_factor
+        value = jnp.where(left, value[:, :rows], value[:, rows:])
+        if shift == 0:
+            keep_ref[...] = value
+        else:
+            send_ref = sends[shift - 1]
+            send_ref[0:feats, :] = value.astype(jnp.bfloat16)
+            put_stats(send_ref, feats, merged[:, :rows])
+            put_stats(send_ref, feats + 48, merged[:, rows:])
+
+
+def finish_kernel(
+    span,
+    pair_total,
+    spot_ref,
+    keep_ref,
+    one_ref,
+    two_ref,
+    three_ref,
+    stats_ref,
+    picked_a_ref,
+    picked_b_ref,
+    picked_c_ref,
+    picked_d_ref,
+    rows_ref,
+    grad_ref,
+    columns_ref,
+    margins_ref,
+):
+    feats, rows = keep_ref.shape
+    place = spot_ref[0] // 4
+    sent = [one_ref, two_ref, three_ref]
+    quads = [stats_ref[...]] + [
+        jnp.concatenate([get_stats(ref, feats), get_stats(ref, feats + 48)], axis=1) for ref in sent
+    ]
+    low = place % 2
+    pair_one = merged_rows(low, quads[0], quads[1])
+    pair_two = merged_rows(low, quads[2], quads[3])
+    final = merged_rows(place // 2, pair_one, pair_two)
+    top, total, target = final[0:1], final[1:2], final[2:3]
+    weights = rows_ref[1:2, :]
+    pair_local = pair_total // 2
+    scored = (target - (top + jnp.log(total))) * weights
+    sequence = lax.broadcasted_iota(jnp.int32, scored.shape, 1) // span
+    lane = lax.broadcasted_iota(jnp.int32, (8, 128), 1)
+    coef = jnp.zeros_like(scored)
+    margins_out = losses_out = jnp.zeros(lane.shape, jnp.float32)
+
+    def lane_of(pair):
+        place = (pair // pair_local) * rows + pair % pair_local
+        return slice(place, place + 1)
+
+    for pair in range(pair_total):
+        sums = [
+            jnp.sum(jnp.where(sequence == 2 * pair + side, scored, 0.0), axis=1, keepdims=True)
+            - rows_ref[3 + side : 4 + side, lane_of(pair)]
+            for side in range(2)
+        ]
+        margin = beta_scale * (sums[0] - sums[1])
+        winner = rows_ref[2:3, lane_of(pair)]
+        loss, slope = pair_terms(margin, winner)
+        scaled = beta_scale * grad_scale / pair_total * slope
+        coef = jnp.where(sequence == 2 * pair, scaled, coef)
+        coef = jnp.where(sequence == 2 * pair + 1, -scaled, coef)
+        margins_out = jnp.where(lane == pair, margin, margins_out)
+        losses_out = jnp.where(lane == pair, loss, losses_out)
+    coef = coef * weights
+    margins_ref[0:8, :] = margins_out
+    margins_ref[8:16, :] = losses_out
+    inverse = 1.0 / total
+    blank = jnp.zeros((5, coef.shape[1]), jnp.float32)
+    columns_ref[...] = jnp.concatenate([coef, top, inverse, blank], axis=0).T
+
+    left = place // 2 == 0
+
+    def own_block(row):
+        return jnp.where(left, row[:, :rows], row[:, rows:])
+
+    value = keep_ref[...] * own_block(jnp.exp(quads[0][0:1] - top))
+    for ref, quad in zip(sent, quads[1:]):
+        value = value + ref[0:feats, :].astype(jnp.float32) * own_block(jnp.exp(quad[0:1] - top))
+    picked = sum(
+        ref[...].astype(jnp.float32)
+        for ref in (picked_a_ref, picked_b_ref, picked_c_ref, picked_d_ref)
+    )
+    picked_coef = coef * (1.0 - jnp.exp(target - top) * inverse)
+    grad_ref[...] = (
+        own_block(picked_coef) * picked
+        - own_block(coef * inverse) * value
+    ).astype(jnp.bfloat16)
+
+
+def small_call(kernel, outs, args):
+    return pl.pallas_call(
+        kernel,
+        out_shape=[jax.ShapeDtypeStruct(shape, dtype) for shape, dtype in outs],
+        in_specs=[pl.BlockSpec(memory_space=pltpu.SMEM)] + vmem_specs(len(args) - 1),
+        out_specs=vmem_specs(len(outs)),
+        compiler_params=pltpu.CompilerParams(vmem_limit_bytes=12 * mebi),
+        cost_estimate=pl.CostEstimate(flops=0, transcendentals=0, bytes_accessed=2000000),
+    )(*args)
+
+
+def finish(grad, stats, picked, rows_info, where, count, span, pair_total):
+    depth, tokens = grad.shape
+    feats = 2 * depth // count
+    rows = tokens // 2
+    f32, bf16 = jnp.float32, jnp.bfloat16
+    half, quarter = depth // 2, depth // 4
+    keep, send = small_call(
+        functools.partial(first_half_kernel, feats),
+        [((half, tokens), f32), ((half + 48, tokens), bf16)],
+        [where, grad, stats],
+    )
+    got = across(send, count, 1)
+    keep, send, stats = small_call(
+        functools.partial(next_half_kernel, feats, 1),
+        [((quarter, tokens), f32), ((quarter + 48, tokens), bf16), ((8, tokens), f32)],
+        [where, keep, got, stats],
+    )
+    got = across(send, count, 2)
+    keep, stats, *sends = small_call(
+        functools.partial(spread_kernel, feats),
+        [((feats, rows), f32), ((8, tokens), f32)] + [((feats + 96, rows), bf16)] * 3,
+        [where, keep, got, stats],
+    )
+    gots = [across(send, count, 4 * shift) for shift, send in zip((1, 2, 3), sends)]
+    return small_call(
+        functools.partial(finish_kernel, span, pair_total),
+        [((feats, rows), bf16), ((tokens, 8), f32), ((16, 128), f32)],
+        [where, keep, *gots, stats, *picked, rows_info],
+    )
+
+
+def head_kernel(first, hidden_ref, logits_ref, rows_ref, target_ref, *rest):
+    out_ref = rest[-1]
+    width = out_ref.shape[1]
+    coef, top, inverse = rows_ref[:, 0:1], rows_ref[:, 1:2], rows_ref[:, 2:3]
+    start = (pl.program_id(0) + first) * width
+    columns = lax.broadcasted_iota(jnp.int32, logits_ref.shape, 1) + start
+    onehot = jnp.where(columns == target_ref[...], 1.0, 0.0)
+    probs = jnp.exp(logits_ref[...] - top) * inverse
+    dlogits = (coef * (onehot - probs)).astype(jnp.bfloat16)
+    depth = out_ref.shape[0]
+    step = 256 if depth % 256 == 0 else depth
+    for start in range(0, depth, step):
+        out_ref[start : start + step, :] = jnp.dot(
+            hidden_ref[start : start + step, :], dlogits, preferred_element_type=jnp.float32
+        ).astype(out_ref.dtype)
+
+
+def head_blocks(hidden_t, logits, row_values, local_targets):
+    depth, tokens = hidden_t.shape
+    cols = logits.shape[1]
+    width = cols // 4 if cols % 512 == 0 else cols
+    steps = cols // width
+    groups = (steps,)
+    out = None
+    first = 0
+    for count in groups:
+        whole = lambda step: (0, 0)
+        column = lambda step, first=first: (0, step + first)
+        in_specs = [
+            pl.BlockSpec((depth, tokens), whole),
+            pl.BlockSpec((tokens, width), column),
+            pl.BlockSpec((tokens, 8), whole),
+            pl.BlockSpec((tokens, 1), whole),
+        ]
+        args = [hidden_t, logits, row_values, local_targets]
+        aliases = {}
+        if out is not None:
+            in_specs.append(pl.BlockSpec(memory_space=pl.ANY))
+            args.append(out)
+            aliases = {4: 0}
+        out = pl.pallas_call(
+            lambda *refs, first=first: head_kernel(first, *refs),
+            out_shape=jax.ShapeDtypeStruct((depth, cols), jnp.bfloat16),
+            grid=(count,),
+            in_specs=in_specs,
+            out_specs=pl.BlockSpec((depth, width), column),
+            input_output_aliases=aliases,
+            compiler_params=pltpu.CompilerParams(vmem_limit_bytes=16 * mebi),
+            cost_estimate=pl.CostEstimate(
+                flops=2 * depth * tokens * width * count,
+                transcendentals=tokens * width * count,
+                bytes_accessed=(2 * depth + 4 * tokens) * width * count,
+            ),
+        )(*args)
+        first += count
+    return out
+
+
+def part_widths(cols):
+    unit = cols // (128 * sum(part_tiles)) * 128
+    if unit == 0 or unit * sum(part_tiles) != cols:
+        return (cols,)
+    return tuple(unit * tile for tile in part_tiles)
+
+
+def paired_local(hidden, head_weight, targets, response_mask, labels, reference_sums):
+    return paired_body(
+        hidden, head_weight, targets, response_mask, labels, reference_sums
+    )
+
+
+def paired_body(hidden, head_weight, targets, response_mask, labels, reference_sums):
+    rows = hidden.shape[0]
+    depth, cols = head_weight.shape
+    pair_local = labels.shape[0]
+    pair_total = 2 * pair_local
+    span = rows // (2 * pair_local)
+    count = lax.axis_size("vocab")
+    half = count // 2
+    plane = lax.axis_index("tok")
+    spot = lax.axis_index("vocab")
+    moves = spot // half != plane
+
+    where = jnp.stack([spot, plane]).astype(jnp.int32)
+    info = jnp.concatenate(
+        [
+            targets.astype(jnp.float32)[None],
+            response_mask.astype(jnp.float32)[None],
+            jnp.pad(labels.astype(jnp.float32)[None], ((0, 0), (0, rows - pair_local))),
+            jnp.pad(reference_sums.T, ((0, 0), (0, rows - pair_local))),
+            jnp.zeros((3, rows), jnp.float32),
+        ],
+        axis=0,
+    )
+    where, moves, info, head_weight = lax.optimization_barrier((where, moves, info, head_weight))
+    piece = plane_swap(hidden.T, count, moves)
+    head_weight = load(head_weight)
+    hidden_t, hidden_n = gather_hidden(piece, where, count)
+    rows_info, local_targets = small_call(
+        functools.partial(side_kernel, cols),
+        [((8, 2 * rows), jnp.float32), ((2 * rows, 1), jnp.int32)],
+        [where, info, over(info)],
+    )
+    picked = pick(where, local_targets, head_weight, count)
+
+    scale = 1.0
+    while hidden_bound * weight_bound * depth * scale > half_limit:
+        scale *= 0.5
+    widths = part_widths(cols)
+    starts = [sum(widths[:part]) for part in range(len(widths))]
+    swapped = []
+    for start, width in zip(starts, widths):
+        own = logit_part(start, width, hidden_n, head_weight)
+        sent = (own * scale if scale != 1.0 else own).astype(jnp.float16)
+        got = over(sent)
+        swapped.append((own, got))
+    logit_parts = []
+    state = None
+    for part, (start, width) in enumerate(zip(starts, widths)):
+        own, got = swapped[part]
+        got = got.astype(jnp.float32)
+        logits = own + (got * (1.0 / scale) if scale != 1.0 else got)
+        logit_parts.append(logits)
+        state = fold(start, width, logits, local_targets, head_weight, state)
+        if part == len(widths) - 2:
+            state, picked = lax.optimization_barrier((state, picked))
+    stats, grad = state
+    hidden_part, row_values, margin_rows = finish(
+        grad, stats, picked, rows_info, where, count, span, pair_total
+    )
+    hidden_grad = plane_swap(hidden_part, count, moves).T
+    other_rows = over(margin_rows)
+    logits = jnp.concatenate(logit_parts, axis=1)
+    head_grad = head_blocks(hidden_t, logits, row_values, local_targets)
+    margins_all = margin_rows[0, :pair_total]
+    margins = jnp.where(plane == 0, margins_all[:pair_local], margins_all[pair_local:])
+    own_losses, other_losses = margin_rows[8], other_rows[8]
+    lane_plane = lax.broadcasted_iota(jnp.int32, (128,), 0) // pair_local
+    losses = jnp.where(lane_plane == plane, own_losses, other_losses)
+    mean_loss = jnp.sum(losses[:pair_total]) / pair_total
+    return (mean_loss, margins, hidden_grad, head_grad)
+
+
 def solution(mesh):
+    count = mesh.shape["vocab"]
+    paired = mesh.shape["tok"] == 2 and count == 16
     return jax.shard_map(
-        local,
+        paired_local if paired else general_local,
         mesh=mesh,
         in_specs=(
             P("tok", "vocab"),

time: 337 us -> 153 us (0.45)
  blocking collectives: 122 us -> 0 us
  waiting for transfers between devices: 110 us -> 58.2 us
  Pallas kernels: 0 us -> 46.3 us
  matrix products: 36.1 us -> 0 us
  starting transfers between devices: 6.04 us -> 33.4 us
  local copies, waits for them, and re-layouts: 29.2 us -> 4.76 us
  between operations: 19.5 us -> 5.96 us
  other arithmetic: 13.5 us -> 3.69 us
    ppermute x0 -> x27, waiting for transfers between devices: none -> 58.2 us  [the longest x9 37.8 us: over(): return lax.ppermute(value, 'tok', swap_pairs)]
    all_to_all x1 -> x0, waiting for transfers between devices: 57.1 us -> none  [local(): lax.all_to_all(partial_value, 'tok', split_axis=0, concat_axis=0, tiled=T...]
    pallas_call x0 -> x25, Pallas kernels: none -> 46.3 us  [the longest x7 11.8 us: fold(): pl.pallas_call(functools.partial(fold_kernel, start, state is not None),...]
    psum x2 -> x0, blocking collectives: 36.3 us -> none  [the longest x1 30.1 us: local(): lax.psum((jnp.sum(shifted, axis=1), local_target), 'vocab')]
    dot_general x3 -> x0, matrix products: 36.1 us -> none  [the longest x1 12.8 us: local(): jnp.dot(token_cols, head_weight, preferred_element_type=jnp.float32)]
    all_gather x1 -> x0, waiting for transfers between devices: 35.2 us -> none  [local(): dlogit_all = lax.all_gather(dlogits, 'tok', axis=0, tiled=True)]
    ppermute x0 -> x27, starting transfers between devices: none -> 33.4 us  [the longest x9 17.1 us: over(): return lax.ppermute(value, 'tok', swap_pairs)]
    all_to_all x2 -> x0, blocking collectives: 30.2 us -> none  [the longest x1 15.4 us: local(): lax.all_to_all(rows_full, 'tok', split_axis=1, concat_axis=0, tiled=True)]
  transfers between devices with their start and end apart: 3 -> 27, of which waited for: 3 -> 11; matrix products, arithmetic and copies ran while one was open for 11% -> 3% of each run, Pallas kernels for 0% -> 27%
where the time goes in v1:
time: 153 us; the launch traced here: 152 us
  waiting for transfers between devices  58.2 us (38%)
  Pallas kernels  46.3 us (30%)
  starting transfers between devices  33.4 us (22%)
  between operations  5.96 us (4%)
  local copies, waits for them, and re-layouts  4.76 us (3%)
  other arithmetic  3.69 us (2%)
    ppermute x9, waiting for transfers between devices, over(): return lax.ppermute(value, 'tok', swap_pairs)  37.8 us
    ppermute x16, waiting for transfers between devices, across(): return lax.ppermute(value, 'vocab', exclusive(count, mask))  20.4 us
    ppermute x9, starting transfers between devices, over(): return lax.ppermute(value, 'tok', swap_pairs)  17.1 us
    ppermute x16, starting transfers between devices, across(): return lax.ppermute(value, 'vocab', exclusive(count, mask))  15 us
    pallas_call x7, Pallas kernels, fold(): pl.pallas_call(functools.partial(fold_kernel, start, state is not None),...  11.8 us
    pallas_call x1, Pallas kernels, head_blocks(): pl.pallas_call(lambda *refs, first=first: head_kernel(first, *refs), out_...  9.72 us
    pallas_call x1, Pallas kernels, pick(): pl.pallas_call(functools.partial(pick_kernel, feats), out_shape=[jax.Shap...  6.41 us
    pallas_call x1, Pallas kernels, load(): pl.pallas_call(load_kernel, out_shape=pltpu.VMEM(head_weight.shape, head_...  6.37 us
  transfers between devices with their start and end apart: 27, of which 11 were waited for; matrix products, arithmetic and copies ran while one was open for 3% of the time, Pallas kernels for 27%

profile of v1, /device:TPU:0, one launch (start us, length us, event | category | flops | bytes accessed | tf_op | source)
XLA Modules:
  0.0 152.3 jit_solution(1207282851963330452)
XLA Ops:
  3.5 6.8 %collective-permute-start.8 = (f32[8,128]{1,0:T(8,128)S(1)}, f32[8,128]{1,0:T(8,128)S(1)}, u32[]{:S(2)}, u32[]{:S(2)}) collective-permute-start(f32[8,128]{1,0:T(8,128)S(1)} %concatenate.9.own_ref), channel_id=1, source_target_pairs={{0,1},{1,0},{2,3},{3,2},{4,5},{5,4},{6,7},{7,6},{8,9},{9,8},{10,11... | collective-permute-start | bytes 12296 | tf_op jit(solution)/shard_map/ppermute | solution.py:107
  10.4 6.4 %shard_map.94.weight_ref = bf16[1792,5120]{1,0:T(8,128)(2,1)S(1)} custom-call(bf16[1792,5120]{1,0:T(8,128)(2,1)} %source_ref), custom_call_target="tpu_custom_call" | custom-call | bytes 18350080 | tf_op jit(solution)/shard_map/pallas_call | solution.py:228
  19.1 2.8 %collective-permute-start.3 = (bf16[224,128]{1,0:T(8,128)(2,1)S(1)}, bf16[224,128]{1,0:T(8,128)(2,1)S(1)}, u32[]{:S(2)}, u32[]{:S(2)}) collective-permute-start(bf16[224,128]{1,0:T(8,128)(2,1)S(1)} %broadcast_select_fusion), channel_id=1, source_target_pairs={{0,24},{2,26},{4,28},{6,30},{8,16},{10,18},{12,20},{14,22},{16,8},... | collective-permute-start | bytes 172040 | tf_op jit(solution)/shard_map/ppermute | solution.py:103
  21.9 6.4 %shard_map.109 = (bf16[896,256]{1,0:T(8,128)(2,1)S(1)}, bf16[896,256]{1,0:T(8,128)(2,1)S(1)}) custom-call(s32[2]{0:T(128)S(1)} %pad_add_fusion.refs_0_.place_ref.spot_ref, s32[256,1]{1,0:T(8,128)S(1)} %get-tuple-element.58.target_ref.refs_3_, bf16[1792,5120]{1,0:T(8,128)(2,1)S(1)} %shard_map.94.weight_ref), custom_call_target="tpu_custom_call" | custom-call | flops 4697620480 | bytes 18350080 | tf_op jit(solution)/shard_map/pallas_call | solution.py:349
  30.3 6.3 %collective-permute-done.4 = bf16[896,128]{1,0:T(8,128)(2,1)S(1)} collective-permute-done((bf16[896,128]{1,0:T(8,128)(2,1)S(1)}, bf16[896,128]{1,0:T(8,128)(2,1)S(1)}, u32[]{:S(2)}, u32[]{:S(2)}) %collective-permute-start.4) | collective-permute-done | bytes 229408 | tf_op jit(solution)/shard_map/ppermute | solution.py:103
  42.4 2.1 %collective-permute-start.13 = (f16[256,512]{1,0:T(8,128)(2,1)S(1)}, f16[256,512]{1,0:T(8,128)(2,1)S(1)}, u32[]{:S(2)}, u32[]{:S(2)}) collective-permute-start(f16[256,512]{1,0:T(8,128)(2,1)S(1)} %convert_element_type.68), channel_id=1, source_target_pairs={{0,1},{1,0},{2,3},{3,2},{4,5},{5,4},{6,7},{7,6},{8,9},{9,8},{10,11... | collective-permute-start | bytes 786440 | tf_op jit(solution)/shard_map/ppermute | solution.py:107
  45.9 2.1 %collective-permute-start.11 = (f16[256,1024]{1,0:T(8,128)(2,1)S(1)}, f16[256,1024]{1,0:T(8,128)(2,1)S(1)}, u32[]{:S(2)}, u32[]{:S(2)}) collective-permute-start(f16[256,1024]{1,0:T(8,128)(2,1)S(1)} %convert_element_type.64), channel_id=1, source_target_pairs={{0,1},{1,0},{2,3},{3,2},{4,5},{5,4},{6,7},{7,6},{8,9},{9,8},{10,11... | collective-permute-start | bytes 1572872 | tf_op jit(solution)/shard_map/ppermute | solution.py:107
  51.5 1.9 %collective-permute-start.9 = (f16[256,512]{1,0:T(8,128)(2,1)S(1)}, f16[256,512]{1,0:T(8,128)(2,1)S(1)}, u32[]{:S(2)}, u32[]{:S(2)}) collective-permute-start(f16[256,512]{1,0:T(8,128)(2,1)S(1)} %convert_element_type.60), channel_id=1, source_target_pairs={{0,1},{1,0},{2,3},{3,2},{4,5},{5,4},{6,7},{7,6},{8,9},{9,8},{10,11... | collective-permute-start | bytes 786440 | tf_op jit(solution)/shard_map/ppermute | solution.py:107
  54.4 2.7 %collective-permute-done.13 = f16[256,512]{1,0:T(8,128)(2,1)S(1)} collective-permute-done((f16[256,512]{1,0:T(8,128)(2,1)S(1)}, f16[256,512]{1,0:T(8,128)(2,1)S(1)}, u32[]{:S(2)}, u32[]{:S(2)}) %collective-permute-start.13) | collective-permute-done | bytes 262176 | tf_op jit(solution)/shard_map/ppermute | solution.py:107
  57.3 1.6 %shard_map.104 = (f32[8,256]{1,0:T(8,128)S(1)}, f32[1792,256]{1,0:T(8,128)S(1)}) custom-call(f32[256,512]{1,0:T(8,128)S(1)} %get-tuple-element.113.logits_ref, s32[256,1]{1,0:T(8,128)S(1)} %get-tuple-element.58.target_ref.refs_3_, bf16[1792,5120]{1,0:T(8,128)(2,1)S(1)} %shard_map.94.weight_ref, ...), custom_call_target="tpu_custom_call", output_to_operand_aliasing={{1}: (4, {})} | custom-call | flops 469762048 | bytes 6029312 | tf_op jit(solution)/shard_map/pallas_call | solution.py:189
  58.9 9.5 %collective-permute-done.12 = f16[256,1024]{1,0:T(8,128)(2,1)S(1)} collective-permute-done((f16[256,1024]{1,0:T(8,128)(2,1)S(1)}, f16[256,1024]{1,0:T(8,128)(2,1)S(1)}, u32[]{:S(2)}, u32[]{:S(2)}) %collective-permute-start.12) | collective-permute-done | bytes 524320 | tf_op jit(solution)/shard_map/ppermute | solution.py:107
  69.3 10.3 %collective-permute-done.11 = f16[256,1024]{1,0:T(8,128)(2,1)S(1)} collective-permute-done((f16[256,1024]{1,0:T(8,128)(2,1)S(1)}, f16[256,1024]{1,0:T(8,128)(2,1)S(1)}, u32[]{:S(2)}, u32[]{:S(2)}) %collective-permute-start.11) | collective-permute-done | bytes 524320 | tf_op jit(solution)/shard_map/ppermute | solution.py:107
  80.1 10.8 %collective-permute-done.10 = f16[256,1024]{1,0:T(8,128)(2,1)S(1)} collective-permute-done((f16[256,1024]{1,0:T(8,128)(2,1)S(1)}, f16[256,1024]{1,0:T(8,128)(2,1)S(1)}, u32[]{:S(2)}, u32[]{:S(2)}) %collective-permute-start.10) | collective-permute-done | bytes 524320 | tf_op jit(solution)/shard_map/ppermute | solution.py:107
  92.2 4.3 %collective-permute-done.9 = f16[256,512]{1,0:T(8,128)(2,1)S(1)} collective-permute-done((f16[256,512]{1,0:T(8,128)(2,1)S(1)}, f16[256,512]{1,0:T(8,128)(2,1)S(1)}, u32[]{:S(2)}, u32[]{:S(2)}) %collective-permute-start.9) | collective-permute-done | bytes 262176 | tf_op jit(solution)/shard_map/ppermute | solution.py:107
  96.6 2.1 %shard_map.105 = (f32[8,256]{1,0:T(8,128)S(1)}, f32[1792,256]{1,0:T(8,128)S(1)}) custom-call(f32[256,1024]{1,0:T(8,128)S(1)} %get-tuple-element.111.logits_ref, s32[256,1]{1,0:T(8,128)S(1)} %get-tuple-element.58.target_ref.refs_3_, bf16[1792,5120]{1,0:T(8,128)(2,1)S(1)} %shard_map.94.weight_ref, ...), custom_call_target="tpu_custom_call", output_to_operand_aliasing={{1}: (4, {})} | custom-call | flops 939524096 | bytes 8388608 | tf_op jit(solution)/shard_map/pallas_call | solution.py:189
  98.7 2.1 %shard_map.106 = (f32[8,256]{1,0:T(8,128)S(1)}, f32[1792,256]{1,0:T(8,128)S(1)}) custom-call(f32[256,1024]{1,0:T(8,128)S(1)} %get-tuple-element.109.logits_ref, s32[256,1]{1,0:T(8,128)S(1)} %get-tuple-element.58.target_ref.refs_3_, bf16[1792,5120]{1,0:T(8,128)(2,1)S(1)} %shard_map.94.weight_ref, ...), custom_call_target="tpu_custom_call", output_to_operand_aliasing={{1}: (4, {})} | custom-call | flops 939524096 | bytes 8388608 | tf_op jit(solution)/shard_map/pallas_call | solution.py:189
  100.9 2.1 %shard_map.107 = (f32[8,256]{1,0:T(8,128)S(1)}, f32[1792,256]{1,0:T(8,128)S(1)}) custom-call(f32[256,1024]{1,0:T(8,128)S(1)} %get-tuple-element.107.logits_ref, s32[256,1]{1,0:T(8,128)S(1)} %get-tuple-element.58.target_ref.refs_3_, bf16[1792,5120]{1,0:T(8,128)(2,1)S(1)} %shard_map.94.weight_ref, ...), custom_call_target="tpu_custom_call", output_to_operand_aliasing={{1}: (4, {})} | custom-call | flops 939524096 | bytes 8388608 | tf_op jit(solution)/shard_map/pallas_call | solution.py:189
  107.7 1.8 %collective-permute-done.20.got_ref = bf16[944,256]{1,0:T(8,128)(2,1)S(1)} collective-permute-done((bf16[944,256]{1,0:T(8,128)(2,1)S(1)}, bf16[944,256]{1,0:T(8,128)(2,1)S(1)}, u32[]{:S(2)}, u32[]{:S(2)}) %collective-permute-start.20) | collective-permute-done | bytes 483360 | tf_op jit(solution)/shard_map/ppermute | solution.py:103
  111.1 7.4 %collective-permute-done.21.got_ref = bf16[496,256]{1,0:T(8,128)(2,1)S(1)} collective-permute-done((bf16[496,256]{1,0:T(8,128)(2,1)S(1)}, bf16[496,256]{1,0:T(8,128)(2,1)S(1)}, u32[]{:S(2)}, u32[]{:S(2)}) %collective-permute-start.21) | collective-permute-done | bytes 253984 | tf_op jit(solution)/shard_map/ppermute | solution.py:103
  120.8 2.8 %collective-permute-start.24 = (bf16[320,128]{1,0:T(8,128)(2,1)S(1)}, bf16[320,128]{1,0:T(8,128)(2,1)S(1)}, u32[]{:S(2)}, u32[]{:S(2)}) collective-permute-start(bf16[320,128]{1,0:T(8,128)(2,1)S(1)} %get-tuple-element.91), channel_id=1, source_target_pairs={{0,24},{2,26},{4,28},{6,30},{8,16},{10,18},{12,20},{14,22},{16,8},... | collective-permute-start | bytes 245768 | tf_op jit(solution)/shard_map/ppermute | solution.py:103
  124.2 4.4 %collective-permute-done.23.two_ref = bf16[320,128]{1,0:T(8,128)(2,1)S(1)} collective-permute-done((bf16[320,128]{1,0:T(8,128)(2,1)S(1)}, bf16[320,128]{1,0:T(8,128)(2,1)S(1)}, u32[]{:S(2)}, u32[]{:S(2)}) %collective-permute-start.23) | collective-permute-done | bytes 81952 | tf_op jit(solution)/shard_map/ppermute | solution.py:103
  130.2 3.9 %collective-permute-start.25 = (f32[16,128]{1,0:T(8,128)S(1)}, f32[16,128]{1,0:T(8,128)S(1)}, u32[]{:S(2)}, u32[]{:S(2)}) collective-permute-start(f32[16,128]{1,0:T(8,128)S(1)} %get-tuple-element.98), channel_id=1, source_target_pairs={{0,1},{1,0},{2,3},{3,2},{4,5},{5,4},{6,7},{7,6},{8,9},{9,8},{10,11... | collective-permute-start | bytes 24584 | tf_op jit(solution)/shard_map/ppermute | solution.py:107
  134.1 2.5 %copy-done.1 = f32[256,5120]{1,0:T(8,128)S(1)} copy-done((f32[256,5120]{1,0:T(8,128)S(1)}, f32[256,5120]{1,0:T(8,128)}, u32[]{:S(2)}) %copy-start.1) | copy-done | bytes 5242904
  136.6 9.7 %shard_map.117 = bf16[1792,5120]{1,0:T(8,128)(2,1)} custom-call(bf16[1792,256]{1,0:T(8,128)(2,1)S(1)} %get-tuple-element.100.refs_0_, f32[256,5120]{1,0:T(8,128)S(1)} %copy-done.1, f32[256,8]{1,0:T(8,128)S(1)} %get-tuple-element.101.refs_2_, s32[256,1]{1,0:T(8,128)S(1)} %get-tuple-element.58.target_ref.refs_3_), custom_call_target="tpu_custom_call" | custom-call | flops 4697620480 | bytes 23592960 | tf_op jit(solution)/shard_map/pallas_call | solution.py:645
  (88 shorter events, 33.4 us)
Async XLA Ops:
  0.6 16.8 %collective-permute-start = (bf16[224,128]{1,0:T(8,128)(2,1)}, bf16[224,128]{1,0:T(8,128)(2,1)S(1)}, u32[]{:S(2)}, u32[]{:S(2)}) collective-permute-start(bf16[224,128]{1,0:T(8,128)(2,1)} %bitcast.29), channel_id=1, source_target_pairs={{16,1},{18,3},{20,5},{22,7},{24,9},{26,11},{28,13},{30,15},{1,16},... | collective-permute-start | bytes 172040 | tf_op jit(solution)/shard_map/ppermute | solution.py:117
  3.5 13.2 %collective-permute-start.8 = (f32[8,128]{1,0:T(8,128)S(1)}, f32[8,128]{1,0:T(8,128)S(1)}, u32[]{:S(2)}, u32[]{:S(2)}) collective-permute-start(f32[8,128]{1,0:T(8,128)S(1)} %concatenate.9.own_ref), channel_id=1, source_target_pairs={{0,1},{1,0},{2,3},{3,2},{4,5},{5,4},{6,7},{7,6},{8,9},{9,8},{10,11... | collective-permute-start | bytes 12296 | tf_op jit(solution)/shard_map/ppermute | solution.py:107
  17.5 10.9 %collective-permute-start.1 = (bf16[224,128]{1,0:T(8,128)(2,1)S(1)}, bf16[224,128]{1,0:T(8,128)(2,1)S(1)}, u32[]{:S(2)}, u32[]{:S(2)}) collective-permute-start(bf16[224,128]{1,0:T(8,128)(2,1)S(1)} %broadcast_select_fusion), channel_id=1, source_target_pairs={{0,8},{2,10},{4,12},{6,14},{8,0},{10,2},{12,4},{14,6},{16,24},{18,... | collective-permute-start | bytes 172040 | tf_op jit(solution)/shard_map/ppermute | solution.py:103
  19.1 9.3 %collective-permute-start.2 = (bf16[224,128]{1,0:T(8,128)(2,1)S(1)}, bf16[224,128]{1,0:T(8,128)(2,1)S(1)}, u32[]{:S(2)}, u32[]{:S(2)}) collective-permute-start(bf16[224,128]{1,0:T(8,128)(2,1)S(1)} %broadcast_select_fusion), channel_id=1, source_target_pairs={{0,16},{2,18},{4,20},{6,22},{8,24},{10,26},{12,28},{14,30},{16,0},... | collective-permute-start | bytes 172040 | tf_op jit(solution)/shard_map/ppermute | solution.py:103
  19.1 9.3 %collective-permute-start.3 = (bf16[224,128]{1,0:T(8,128)(2,1)S(1)}, bf16[224,128]{1,0:T(8,128)(2,1)S(1)}, u32[]{:S(2)}, u32[]{:S(2)}) collective-permute-start(bf16[224,128]{1,0:T(8,128)(2,1)S(1)} %broadcast_select_fusion), channel_id=1, source_target_pairs={{0,24},{2,26},{4,28},{6,30},{8,16},{10,18},{12,20},{14,22},{16,8},... | collective-permute-start | bytes 172040 | tf_op jit(solution)/shard_map/ppermute | solution.py:103
  28.3 8.2 %collective-permute-start.15 = (bf16[896,256]{1,0:T(8,128)(2,1)S(1)}, bf16[896,256]{1,0:T(8,128)(2,1)S(1)}, u32[]{:S(2)}, u32[]{:S(2)}) collective-permute-start(bf16[896,256]{1,0:T(8,128)(2,1)S(1)} %get-tuple-element.72), channel_id=1, source_target_pairs={{0,2},{2,0},{4,6},{6,4},{8,10},{10,8},{12,14},{14,12},{16,18},{18,... | collective-permute-start | bytes 1376264 | tf_op jit(solution)/shard_map/ppermute | solution.py:103
  28.5 8.1 %collective-permute-start.4 = (bf16[896,128]{1,0:T(8,128)(2,1)S(1)}, bf16[896,128]{1,0:T(8,128)(2,1)S(1)}, u32[]{:S(2)}, u32[]{:S(2)}) collective-permute-start(bf16[896,128]{1,0:T(8,128)(2,1)S(1)} %pad_maximum_fusion), channel_id=1, source_target_pairs={{0,4},{2,6},{4,0},{6,2},{8,12},{10,14},{12,8},{14,10},{16,20},{18,... | collective-permute-start | bytes 688136 | tf_op jit(solution)/shard_map/ppermute | solution.py:103
  30.1 8.7 %collective-permute-start.5 = (bf16[896,128]{1,0:T(8,128)(2,1)S(1)}, bf16[896,128]{1,0:T(8,128)(2,1)S(1)}, u32[]{:S(2)}, u32[]{:S(2)}) collective-permute-start(bf16[896,128]{1,0:T(8,128)(2,1)S(1)} %pad_maximum_fusion), channel_id=1, source_target_pairs={{0,2},{2,0},{4,6},{6,4},{8,10},{10,8},{12,14},{14,12},{16,18},{18,... | collective-permute-start | bytes 688136 | tf_op jit(solution)/shard_map/ppermute | solution.py:103
  37.1 13.4 %collective-permute-start.16 = (bf16[448,256]{1,0:T(8,128)(2,1)S(1)}, bf16[448,256]{1,0:T(8,128)(2,1)S(1)}, u32[]{:S(2)}, u32[]{:S(2)}) collective-permute-start(bf16[448,256]{1,0:T(8,128)(2,1)S(1)} %get-tuple-element.74), channel_id=1, source_target_pairs={{0,4},{2,6},{4,0},{6,2},{8,12},{10,14},{12,8},{14,10},{16,20},{18,... | collective-permute-start | bytes 688136 | tf_op jit(solution)/shard_map/ppermute | solution.py:103
  42.3 9.2 %collective-permute-start.14 = (f16[256,512]{1,0:T(8,128)(2,1)S(1)}, f16[256,512]{1,0:T(8,128)(2,1)S(1)}, u32[]{:S(2)}, u32[]{:S(2)}) collective-permute-start(f16[256,512]{1,0:T(8,128)(2,1)S(1)} %convert_element_type.70), channel_id=1, source_target_pairs={{0,1},{1,0},{2,3},{3,2},{4,5},{5,4},{6,7},{7,6},{8,9},{9,8},{10,11... | collective-permute-start | bytes 786440 | tf_op jit(solution)/shard_map/ppermute | solution.py:107
  42.4 14.7 %collective-permute-start.13 = (f16[256,512]{1,0:T(8,128)(2,1)S(1)}, f16[256,512]{1,0:T(8,128)(2,1)S(1)}, u32[]{:S(2)}, u32[]{:S(2)}) collective-permute-start(f16[256,512]{1,0:T(8,128)(2,1)S(1)} %convert_element_type.68), channel_id=1, source_target_pairs={{0,1},{1,0},{2,3},{3,2},{4,5},{5,4},{6,7},{7,6},{8,9},{9,8},{10,11... | collective-permute-start | bytes 786440 | tf_op jit(solution)/shard_map/ppermute | solution.py:107
  44.6 23.8 %collective-permute-start.12 = (f16[256,1024]{1,0:T(8,128)(2,1)S(1)}, f16[256,1024]{1,0:T(8,128)(2,1)S(1)}, u32[]{:S(2)}, u32[]{:S(2)}) collective-permute-start(f16[256,1024]{1,0:T(8,128)(2,1)S(1)} %convert_element_type.66), channel_id=1, source_target_pairs={{0,1},{1,0},{2,3},{3,2},{4,5},{5,4},{6,7},{7,6},{8,9},{9,8},{10,11... | collective-permute-start | bytes 1572872 | tf_op jit(solution)/shard_map/ppermute | solution.py:107
  45.9 33.8 %collective-permute-start.11 = (f16[256,1024]{1,0:T(8,128)(2,1)S(1)}, f16[256,1024]{1,0:T(8,128)(2,1)S(1)}, u32[]{:S(2)}, u32[]{:S(2)}) collective-permute-start(f16[256,1024]{1,0:T(8,128)(2,1)S(1)} %convert_element_type.64), channel_id=1, source_target_pairs={{0,1},{1,0},{2,3},{3,2},{4,5},{5,4},{6,7},{7,6},{8,9},{9,8},{10,11... | collective-permute-start | bytes 1572872 | tf_op jit(solution)/shard_map/ppermute | solution.py:107
  50.6 40.3 %collective-permute-start.10 = (f16[256,1024]{1,0:T(8,128)(2,1)S(1)}, f16[256,1024]{1,0:T(8,128)(2,1)S(1)}, u32[]{:S(2)}, u32[]{:S(2)}) collective-permute-start(f16[256,1024]{1,0:T(8,128)(2,1)S(1)} %convert_element_type.62), channel_id=1, source_target_pairs={{0,1},{1,0},{2,3},{3,2},{4,5},{5,4},{6,7},{7,6},{8,9},{9,8},{10,11... | collective-permute-start | bytes 1572872 | tf_op jit(solution)/shard_map/ppermute | solution.py:107
  51.5 44.9 %collective-permute-start.9 = (f16[256,512]{1,0:T(8,128)(2,1)S(1)}, f16[256,512]{1,0:T(8,128)(2,1)S(1)}, u32[]{:S(2)}, u32[]{:S(2)}) collective-permute-start(f16[256,512]{1,0:T(8,128)(2,1)S(1)} %convert_element_type.60), channel_id=1, source_target_pairs={{0,1},{1,0},{2,3},{3,2},{4,5},{5,4},{6,7},{7,6},{8,9},{9,8},{10,11... | collective-permute-start | bytes 786440 | tf_op jit(solution)/shard_map/ppermute | solution.py:107
  57.2 47.3 %collective-permute-start.7 = (f16[256,512]{1,0:T(8,128)(2,1)S(1)}, f16[256,512]{1,0:T(8,128)(2,1)S(1)}, u32[]{:S(2)}, u32[]{:S(2)}) collective-permute-start(f16[256,512]{1,0:T(8,128)(2,1)S(1)} %convert_element_type.58), channel_id=1, source_target_pairs={{0,1},{1,0},{2,3},{3,2},{4,5},{5,4},{6,7},{7,6},{8,9},{9,8},{10,11... | collective-permute-start | bytes 786440 | tf_op jit(solution)/shard_map/ppermute | solution.py:107
  68.4 36.1 %collective-permute-start.17 = (bf16[224,128]{1,0:T(8,128)(2,1)S(1)}, bf16[224,128]{1,0:T(8,128)(2,1)S(1)}, u32[]{:S(2)}, u32[]{:S(2)}) collective-permute-start(bf16[224,128]{1,0:T(8,128)(2,1)S(1)} %get-tuple-element.76), channel_id=1, source_target_pairs={{0,8},{2,10},{4,12},{6,14},{8,0},{10,2},{12,4},{14,6},{16,24},{18,... | collective-permute-start | bytes 172040 | tf_op jit(solution)/shard_map/ppermute | solution.py:103
  79.6 24.8 %collective-permute-start.18 = (bf16[224,128]{1,0:T(8,128)(2,1)S(1)}, bf16[224,128]{1,0:T(8,128)(2,1)S(1)}, u32[]{:S(2)}, u32[]{:S(2)}) collective-permute-start(bf16[224,128]{1,0:T(8,128)(2,1)S(1)} %get-tuple-element.77), channel_id=1, source_target_pairs={{0,16},{2,18},{4,20},{6,22},{8,24},{10,26},{12,28},{14,30},{16,0},... | collective-permute-start | bytes 172040 | tf_op jit(solution)/shard_map/ppermute | solution.py:103
  90.9 13.6 %collective-permute-start.19 = (bf16[224,128]{1,0:T(8,128)(2,1)S(1)}, bf16[224,128]{1,0:T(8,128)(2,1)S(1)}, u32[]{:S(2)}, u32[]{:S(2)}) collective-permute-start(bf16[224,128]{1,0:T(8,128)(2,1)S(1)} %get-tuple-element.78), channel_id=1, source_target_pairs={{0,24},{2,26},{4,28},{6,30},{8,16},{10,18},{12,20},{14,22},{16,8},... | collective-permute-start | bytes 172040 | tf_op jit(solution)/shard_map/ppermute | solution.py:103
  110.2 8.2 %collective-permute-start.21 = (bf16[496,256]{1,0:T(8,128)(2,1)S(1)}, bf16[496,256]{1,0:T(8,128)(2,1)S(1)}, u32[]{:S(2)}, u32[]{:S(2)}) collective-permute-start(bf16[496,256]{1,0:T(8,128)(2,1)S(1)} %get-tuple-element.86), channel_id=1, source_target_pairs={{0,4},{2,6},{4,0},{6,2},{8,12},{10,14},{12,8},{14,10},{16,20},{18,... | collective-permute-start | bytes 761864 | tf_op jit(solution)/shard_map/ppermute | solution.py:103
  119.9 8.6 %collective-permute-start.23 = (bf16[320,128]{1,0:T(8,128)(2,1)S(1)}, bf16[320,128]{1,0:T(8,128)(2,1)S(1)}, u32[]{:S(2)}, u32[]{:S(2)}) collective-permute-start(bf16[320,128]{1,0:T(8,128)(2,1)S(1)} %get-tuple-element.90), channel_id=1, source_target_pairs={{0,16},{2,18},{4,20},{6,22},{8,24},{10,26},{12,28},{14,30},{16,0},... | collective-permute-start | bytes 245768 | tf_op jit(solution)/shard_map/ppermute | solution.py:103
  120.8 7.8 %collective-permute-start.24 = (bf16[320,128]{1,0:T(8,128)(2,1)S(1)}, bf16[320,128]{1,0:T(8,128)(2,1)S(1)}, u32[]{:S(2)}, u32[]{:S(2)}) collective-permute-start(bf16[320,128]{1,0:T(8,128)(2,1)S(1)} %get-tuple-element.91), channel_id=1, source_target_pairs={{0,24},{2,26},{4,28},{6,30},{8,16},{10,18},{12,20},{14,22},{16,8},... | collective-permute-start | bytes 245768 | tf_op jit(solution)/shard_map/ppermute | solution.py:103
  129.5 19.9 %collective-permute-start.26 = (bf16[224,128]{1,0:T(8,128)(2,1)S(1)}, bf16[224,128]{1,0:T(8,128)(2,1)S(1)}, u32[]{:S(2)}, u32[]{:S(2)}) collective-permute-start(bf16[224,128]{1,0:T(8,128)(2,1)S(1)} %get-tuple-element.99), channel_id=1, source_target_pairs={{16,1},{18,3},{20,5},{22,7},{24,9},{26,11},{28,13},{30,15},{1,16},... | collective-permute-start | bytes 172040 | tf_op jit(solution)/shard_map/ppermute | solution.py:117
  130.2 18.0 %collective-permute-start.25 = (f32[16,128]{1,0:T(8,128)S(1)}, f32[16,128]{1,0:T(8,128)S(1)}, u32[]{:S(2)}, u32[]{:S(2)}) collective-permute-start(f32[16,128]{1,0:T(8,128)S(1)} %get-tuple-element.98), channel_id=1, source_target_pairs={{0,1},{1,0},{2,3},{3,2},{4,5},{5,4},{6,7},{7,6},{8,9},{9,8},{10,11... | collective-permute-start | bytes 24584 | tf_op jit(solution)/shard_map/ppermute | solution.py:107
  (6 other events, 27.9 us)

commit v2 on v1

--- a/solution.py
+++ b/solution.py
@@ -93,6 +93,7 @@
 half_limit = 60000.0
 part_tiles = (4, 4, 8, 8, 8, 4, 4)
 mebi = 1 << 20
+stats_rows = 16
 
 
 def exclusive(count, mask):
@@ -115,7 +116,7 @@
             if spot // half != plane:
                 pairs.append((2 * spot + plane, 2 * (spot ^ half) + 1 - plane))
     received = lax.ppermute(value, ("vocab", "tok"), pairs)
-    return jnp.where(moves, received, value)
+    return received if moves is None else jnp.where(moves, received, value)
 
 
 def place_kernel(order, spot_ref, *refs):
@@ -388,25 +389,20 @@
     return [pl.BlockSpec(memory_space=pltpu.VMEM)] * number
 
 
-def split_rows(rows):
-    high = rows.astype(jnp.bfloat16)
-    rest = rows - high.astype(jnp.float32)
-    middle = rest.astype(jnp.bfloat16)
-    low = (rest - middle.astype(jnp.float32)).astype(jnp.bfloat16)
-    return [high, middle, low]
-
-
 def put_stats(ref, start, rows):
-    for index, block in enumerate(split_rows(jnp.concatenate([rows, rows], axis=0))):
-        ref[start + 16 * index : start + 16 * index + 16, :] = block
+    rows = rows[0:3]
+    high = rows.astype(jnp.bfloat16).astype(jnp.float32)
+    rest = rows - high
+    middle = rest.astype(jnp.bfloat16).astype(jnp.float32)
+    blank = jnp.zeros((stats_rows - 9, rows.shape[1]), jnp.float32)
+    block = jnp.concatenate([high, middle, rest - middle, blank], axis=0)
+    ref[start : start + stats_rows, :] = block.astype(jnp.bfloat16)
 
 
 def get_stats(ref, start):
-    blocks = [
-        ref[start + 16 * index : start + 16 * index + 16, :].astype(jnp.float32)[0:8]
-        for index in range(3)
-    ]
-    return blocks[0] + blocks[1] + blocks[2]
+    block = ref[start : start + stats_rows, :].astype(jnp.float32)
+    blank = jnp.zeros((5, block.shape[1]), jnp.float32)
+    return jnp.concatenate([block[0:3] + block[3:6] + block[6:9], blank], axis=0)
 
 
 def merged_rows(bit, own, other):
@@ -476,7 +472,7 @@
             send_ref = sends[shift - 1]
             send_ref[0:feats, :] = value.astype(jnp.bfloat16)
             put_stats(send_ref, feats, merged[:, :rows])
-            put_stats(send_ref, feats + 48, merged[:, rows:])
+            put_stats(send_ref, feats + stats_rows, merged[:, rows:])
 
 
 def finish_kernel(
@@ -501,7 +497,7 @@
     place = spot_ref[0] // 4
     sent = [one_ref, two_ref, three_ref]
     quads = [stats_ref[...]] + [
-        jnp.concatenate([get_stats(ref, feats), get_stats(ref, feats + 48)], axis=1) for ref in sent
+        jnp.concatenate([get_stats(ref, feats), get_stats(ref, feats + stats_rows)], axis=1) for ref in sent
     ]
     low = place % 2
     pair_one = merged_rows(low, quads[0], quads[1])
@@ -579,19 +575,19 @@
     half, quarter = depth // 2, depth // 4
     keep, send = small_call(
         functools.partial(first_half_kernel, feats),
-        [((half, tokens), f32), ((half + 48, tokens), bf16)],
+        [((half, tokens), f32), ((half + stats_rows, tokens), bf16)],
         [where, grad, stats],
     )
     got = across(send, count, 1)
     keep, send, stats = small_call(
         functools.partial(next_half_kernel, feats, 1),
-        [((quarter, tokens), f32), ((quarter + 48, tokens), bf16), ((8, tokens), f32)],
+        [((quarter, tokens), f32), ((quarter + stats_rows, tokens), bf16), ((8, tokens), f32)],
         [where, keep, got, stats],
     )
     got = across(send, count, 2)
     keep, stats, *sends = small_call(
         functools.partial(spread_kernel, feats),
-        [((feats, rows), f32), ((8, tokens), f32)] + [((feats + 96, rows), bf16)] * 3,
+        [((feats, rows), f32), ((8, tokens), f32)] + [((feats + 2 * stats_rows, rows), bf16)] * 3,
         [where, keep, got, stats],
     )
     gots = [across(send, count, 4 * shift) for shift, send in zip((1, 2, 3), sends)]
@@ -602,62 +598,70 @@
     )
 
 
-def head_kernel(first, hidden_ref, logits_ref, rows_ref, target_ref, *rest):
-    out_ref = rest[-1]
+def head_kernel(hidden_ref, logits_ref, rows_ref, target_ref, out_ref):
     width = out_ref.shape[1]
     coef, top, inverse = rows_ref[:, 0:1], rows_ref[:, 1:2], rows_ref[:, 2:3]
-    start = (pl.program_id(0) + first) * width
-    columns = lax.broadcasted_iota(jnp.int32, logits_ref.shape, 1) + start
-    onehot = jnp.where(columns == target_ref[...], 1.0, 0.0)
-    probs = jnp.exp(logits_ref[...] - top) * inverse
-    dlogits = (coef * (onehot - probs)).astype(jnp.bfloat16)
     depth = out_ref.shape[0]
-    step = 256 if depth % 256 == 0 else depth
-    for start in range(0, depth, step):
-        out_ref[start : start + step, :] = jnp.dot(
-            hidden_ref[start : start + step, :], dlogits, preferred_element_type=jnp.float32
-        ).astype(out_ref.dtype)
+    rows = 256 if depth % 256 == 0 else depth
+    part = 256 if width % 256 == 0 else width
+    columns = lax.broadcasted_iota(jnp.int32, (logits_ref.shape[0], part), 1)
+    start = pl.program_id(0) * width
+    for column in range(0, width, part):
+        onehot = jnp.where(columns + (start + column) == target_ref[...], 1.0, 0.0)
+        probs = jnp.exp(logits_ref[:, column : column + part] - top) * inverse
+        dlogits = (coef * (onehot - probs)).astype(jnp.bfloat16)
+        for first in range(0, depth, rows):
+            out_ref[first : first + rows, column : column + part] = jnp.dot(
+                hidden_ref[first : first + rows, :],
+                dlogits,
+                preferred_element_type=jnp.float32,
+            ).astype(out_ref.dtype)
 
 
 def head_blocks(hidden_t, logits, row_values, local_targets):
     depth, tokens = hidden_t.shape
     cols = logits.shape[1]
-    width = cols // 4 if cols % 512 == 0 else cols
-    steps = cols // width
-    groups = (steps,)
-    out = None
-    first = 0
-    for count in groups:
-        whole = lambda step: (0, 0)
-        column = lambda step, first=first: (0, step + first)
-        in_specs = [
+    width = cols // 5 if cols % (5 * 256) == 0 else cols
+    whole = lambda step: (0, 0)
+    column = lambda step: (0, step)
+    return pl.pallas_call(
+        head_kernel,
+        out_shape=jax.ShapeDtypeStruct((depth, cols), jnp.bfloat16),
+        grid=(cols // width,),
+        in_specs=[
             pl.BlockSpec((depth, tokens), whole),
             pl.BlockSpec((tokens, width), column),
             pl.BlockSpec((tokens, 8), whole),
             pl.BlockSpec((tokens, 1), whole),
-        ]
-        args = [hidden_t, logits, row_values, local_targets]
-        aliases = {}
-        if out is not None:
-            in_specs.append(pl.BlockSpec(memory_space=pl.ANY))
-            args.append(out)
-            aliases = {4: 0}
-        out = pl.pallas_call(
-            lambda *refs, first=first: head_kernel(first, *refs),
-            out_shape=jax.ShapeDtypeStruct((depth, cols), jnp.bfloat16),
-            grid=(count,),
-            in_specs=in_specs,
-            out_specs=pl.BlockSpec((depth, width), column),
-            input_output_aliases=aliases,
-            compiler_params=pltpu.CompilerParams(vmem_limit_bytes=16 * mebi),
-            cost_estimate=pl.CostEstimate(
-                flops=2 * depth * tokens * width * count,
-                transcendentals=tokens * width * count,
-                bytes_accessed=(2 * depth + 4 * tokens) * width * count,
-            ),
-        )(*args)
-        first += count
-    return out
+        ],
+        out_specs=pl.BlockSpec((depth, width), column),
+        compiler_params=pltpu.CompilerParams(vmem_limit_bytes=40 * mebi),
+        cost_estimate=pl.CostEstimate(
+            flops=2 * depth * tokens * cols,
+            transcendentals=tokens * cols,
+            bytes_accessed=(2 * depth + 4 * tokens) * cols,
+        ),
+    )(hidden_t, logits, row_values, local_targets)
+
+
+def last_kernel(pair_local, place_ref, rows_ref, other_ref, own_ref, got_ref, grad_ref, loss_ref, margin_ref):
+    half = place_ref[2]
+    plane = place_ref[1]
+    first = plane == 0
+    moved = jnp.where(
+        place_ref[0] // half != plane,
+        got_ref[...].astype(jnp.float32),
+        own_ref[...].astype(jnp.float32),
+    )
+    grad_ref[...] = moved.astype(grad_ref.dtype)
+    total = jnp.zeros((1, 1), jnp.float32)
+    for pair in range(2 * pair_local):
+        own, other = rows_ref[8:9, pair : pair + 1], other_ref[8:9, pair : pair + 1]
+        total = total + jnp.where(first == (pair < pair_local), own, other)
+    loss_ref[...] = total / (2 * pair_local)
+    margin_ref[...] = jnp.where(
+        first, rows_ref[0:1, 0:pair_local], rows_ref[0:1, pair_local : 2 * pair_local]
+    )
 
 
 def part_widths(cols):
@@ -685,7 +689,7 @@
     spot = lax.axis_index("vocab")
     moves = spot // half != plane
 
-    where = jnp.stack([spot, plane]).astype(jnp.int32)
+    where = jnp.stack([spot, plane, jnp.full_like(spot, half)]).astype(jnp.int32)
     info = jnp.concatenate(
         [
             targets.astype(jnp.float32)[None],
@@ -726,22 +730,21 @@
         logits = own + (got * (1.0 / scale) if scale != 1.0 else got)
         logit_parts.append(logits)
         state = fold(start, width, logits, local_targets, head_weight, state)
-        if part == len(widths) - 2:
-            state, picked = lax.optimization_barrier((state, picked))
     stats, grad = state
     hidden_part, row_values, margin_rows = finish(
         grad, stats, picked, rows_info, where, count, span, pair_total
     )
-    hidden_grad = plane_swap(hidden_part, count, moves).T
+    hidden_got = plane_swap(hidden_part, count, None)
     other_rows = over(margin_rows)
     logits = jnp.concatenate(logit_parts, axis=1)
     head_grad = head_blocks(hidden_t, logits, row_values, local_targets)
-    margins_all = margin_rows[0, :pair_total]
-    margins = jnp.where(plane == 0, margins_all[:pair_local], margins_all[pair_local:])
-    own_losses, other_losses = margin_rows[8], other_rows[8]
-    lane_plane = lax.broadcasted_iota(jnp.int32, (128,), 0) // pair_local
-    losses = jnp.where(lane_plane == plane, own_losses, other_losses)
-    mean_loss = jnp.sum(losses[:pair_total]) / pair_total
+    hidden_grad_t, mean_loss, margins = small_call(
+        functools.partial(last_kernel, pair_local),
+        [(hidden_part.shape, hidden.dtype), ((1, 1), jnp.float32), ((1, pair_local), jnp.float32)],
+        [where, margin_rows, other_rows, hidden_part, hidden_got],
+    )
+    hidden_grad = hidden_grad_t.T
+    mean_loss, margins = mean_loss.reshape(()), margins.reshape(pair_local)
     return (mean_loss, margins, hidden_grad, head_grad)
 
 

time: 153 us -> 148 us (0.967)
  between operations: 5.96 us -> 1.71 us
  starting transfers between devices: 33.4 us -> 37.4 us
  local copies, waits for them, and re-layouts: 4.76 us -> 0.78 us
    ppermute x16, starting transfers between devices: 15 us -> 21.4 us  [across(): return lax.ppermute(value, 'vocab', exclusive(count, mask))]
    ppermute x9, waiting for transfers between devices: 37.8 us -> 33.9 us  [over(): return lax.ppermute(value, 'tok', swap_pairs)]
    unnamed x6 -> x0, local copies, waits for them, and re-layouts: 3.39 us -> none
    ppermute x16, waiting for transfers between devices: 20.4 us -> 23.3 us  [across(): return lax.ppermute(value, 'vocab', exclusive(count, mask))]
    ppermute x9, starting transfers between devices: 17.1 us -> 14.7 us  [over(): return lax.ppermute(value, 'tok', swap_pairs)]
    pallas_call x7 -> x8, Pallas kernels: 4.96 us -> 6.15 us  [small_call(): pl.pallas_call(kernel, out_shape=[jax.ShapeDtypeStruct(shape, dtype) for...]
  transfers between devices with their start and end apart: 27 -> 27, of which waited for: 11 -> 12; matrix products, arithmetic and copies ran while one was open for 3% -> 2% of each run, Pallas kernels for 27% -> 31%
where the time goes in v2:
time: 148 us
  waiting for transfers between devices  57.3 us (39%)
  Pallas kernels  47.7 us (32%)
  starting transfers between devices  37.4 us (25%)
  other arithmetic  2.93 us (2%)
  between operations  1.71 us (1%)
    ppermute x9, waiting for transfers between devices, over(): return lax.ppermute(value, 'tok', swap_pairs)  33.9 us
    ppermute x16, waiting for transfers between devices, across(): return lax.ppermute(value, 'vocab', exclusive(count, mask))  23.3 us
    ppermute x16, starting transfers between devices, across(): return lax.ppermute(value, 'vocab', exclusive(count, mask))  21.4 us
    ppermute x9, starting transfers between devices, over(): return lax.ppermute(value, 'tok', swap_pairs)  14.7 us
    pallas_call x7, Pallas kernels, fold(): pl.pallas_call(functools.partial(fold_kernel, start, state is not None),...  11.8 us
    pallas_call x1, Pallas kernels, head_blocks(): pl.pallas_call(head_kernel, out_shape=jax.ShapeDtypeStruct((depth, cols),...  9.95 us
    pallas_call x1, Pallas kernels, pick(): pl.pallas_call(functools.partial(pick_kernel, feats), out_shape=[jax.Shap...  6.4 us
    pallas_call x1, Pallas kernels, load(): pl.pallas_call(load_kernel, out_shape=pltpu.VMEM(head_weight.shape, head_...  6.37 us
  transfers between devices with their start and end apart: 27, of which 12 were waited for; matrix products, arithmetic and copies ran while one was open for 2% of the time, Pallas kernels for 31%

profile of v2, /device:TPU:0, one launch (start us, length us, event | category | flops | bytes accessed | tf_op | source)
XLA Modules:
  0.0 147.8 jit_solution(5030573359014493354)
XLA Ops:
  4.4 3.1 %collective-permute-start.1 = (bf16[224,128]{1,0:T(8,128)(2,1)S(1)}, bf16[224,128]{1,0:T(8,128)(2,1)S(1)}, u32[]{:S(2)}, u32[]{:S(2)}) collective-permute-start(bf16[224,128]{1,0:T(8,128)(2,1)S(1)} %broadcast_select_fusion), channel_id=1, source_target_pairs={{0,8},{2,10},{4,12},{6,14},{8,0},{10,2},{12,4},{14,6},{16,24},{18,... | collective-permute-start | bytes 172040 | tf_op jit(solution)/shard_map/ppermute | solution.py:104
  7.4 8.4 %collective-permute-start.2 = (bf16[224,128]{1,0:T(8,128)(2,1)S(1)}, bf16[224,128]{1,0:T(8,128)(2,1)S(1)}, u32[]{:S(2)}, u32[]{:S(2)}) collective-permute-start(bf16[224,128]{1,0:T(8,128)(2,1)S(1)} %broadcast_select_fusion), channel_id=1, source_target_pairs={{0,16},{2,18},{4,20},{6,22},{8,24},{10,26},{12,28},{14,30},{16,0},... | collective-permute-start | bytes 172040 | tf_op jit(solution)/shard_map/ppermute | solution.py:104
  15.8 3.4 %collective-permute-done.2 = bf16[224,128]{1,0:T(8,128)(2,1)S(1)} collective-permute-done((bf16[224,128]{1,0:T(8,128)(2,1)S(1)}, bf16[224,128]{1,0:T(8,128)(2,1)S(1)}, u32[]{:S(2)}, u32[]{:S(2)}) %collective-permute-start.2) | collective-permute-done | bytes 57376 | tf_op jit(solution)/shard_map/ppermute | solution.py:104
  19.2 2.6 %collective-permute-done.3 = bf16[224,128]{1,0:T(8,128)(2,1)S(1)} collective-permute-done((bf16[224,128]{1,0:T(8,128)(2,1)S(1)}, bf16[224,128]{1,0:T(8,128)(2,1)S(1)}, u32[]{:S(2)}, u32[]{:S(2)}) %collective-permute-start.3) | collective-permute-done | bytes 57376 | tf_op jit(solution)/shard_map/ppermute | solution.py:104
  23.4 6.4 %shard_map.94.weight_ref = bf16[1792,5120]{1,0:T(8,128)(2,1)S(1)} custom-call(bf16[1792,5120]{1,0:T(8,128)(2,1)} %source_ref), custom_call_target="tpu_custom_call" | custom-call | bytes 18350080 | tf_op jit(solution)/shard_map/pallas_call | solution.py:229
  31.1 6.4 %shard_map.113 = (bf16[896,256]{1,0:T(8,128)(2,1)S(1)}, bf16[896,256]{1,0:T(8,128)(2,1)S(1)}) custom-call(s32[3]{0:T(128)S(1)} %pad_add_fusion.refs_0_.place_ref.spot_ref, s32[256,1]{1,0:T(8,128)S(1)} %get-tuple-element.55.target_ref, bf16[1792,5120]{1,0:T(8,128)(2,1)S(1)} %shard_map.94.weight_ref), custom_call_target="tpu_custom_call" | custom-call | flops 4697620480 | bytes 18350080 | tf_op jit(solution)/shard_map/pallas_call | solution.py:350
  41.1 2.1 %collective-permute-start.14 = (f16[256,512]{1,0:T(8,128)(2,1)S(1)}, f16[256,512]{1,0:T(8,128)(2,1)S(1)}, u32[]{:S(2)}, u32[]{:S(2)}) collective-permute-start(f16[256,512]{1,0:T(8,128)(2,1)S(1)} %convert_element_type.70), channel_id=1, source_target_pairs={{0,1},{1,0},{2,3},{3,2},{4,5},{5,4},{6,7},{7,6},{8,9},{9,8},{10,11... | collective-permute-start | bytes 786440 | tf_op jit(solution)/shard_map/ppermute | solution.py:108
  43.4 2.1 %collective-permute-start.12 = (f16[256,1024]{1,0:T(8,128)(2,1)S(1)}, f16[256,1024]{1,0:T(8,128)(2,1)S(1)}, u32[]{:S(2)}, u32[]{:S(2)}) collective-permute-start(f16[256,1024]{1,0:T(8,128)(2,1)S(1)} %convert_element_type.66), channel_id=1, source_target_pairs={{0,1},{1,0},{2,3},{3,2},{4,5},{5,4},{6,7},{7,6},{8,9},{9,8},{10,11... | collective-permute-start | bytes 1572872 | tf_op jit(solution)/shard_map/ppermute | solution.py:108
  50.4 2.0 %collective-permute-start.10 = (f16[256,1024]{1,0:T(8,128)(2,1)S(1)}, f16[256,1024]{1,0:T(8,128)(2,1)S(1)}, u32[]{:S(2)}, u32[]{:S(2)}) collective-permute-start(f16[256,1024]{1,0:T(8,128)(2,1)S(1)} %convert_element_type.62), channel_id=1, source_target_pairs={{0,1},{1,0},{2,3},{3,2},{4,5},{5,4},{6,7},{7,6},{8,9},{9,8},{10,11... | collective-permute-start | bytes 1572872 | tf_op jit(solution)/shard_map/ppermute | solution.py:108
  53.4 2.6 %collective-permute-done.13 = f16[256,512]{1,0:T(8,128)(2,1)S(1)} collective-permute-done((f16[256,512]{1,0:T(8,128)(2,1)S(1)}, f16[256,512]{1,0:T(8,128)(2,1)S(1)}, u32[]{:S(2)}, u32[]{:S(2)}) %collective-permute-start.13) | collective-permute-done | bytes 262176 | tf_op jit(solution)/shard_map/ppermute | solution.py:108
  59.8 7.5 %collective-permute-done.12 = f16[256,1024]{1,0:T(8,128)(2,1)S(1)} collective-permute-done((f16[256,1024]{1,0:T(8,128)(2,1)S(1)}, f16[256,1024]{1,0:T(8,128)(2,1)S(1)}, u32[]{:S(2)}, u32[]{:S(2)}) %collective-permute-start.12) | collective-permute-done | bytes 524320 | tf_op jit(solution)/shard_map/ppermute | solution.py:108
  67.2 2.0 %collective-permute-start.7 = (f16[256,512]{1,0:T(8,128)(2,1)S(1)}, f16[256,512]{1,0:T(8,128)(2,1)S(1)}, u32[]{:S(2)}, u32[]{:S(2)}) collective-permute-start(f16[256,512]{1,0:T(8,128)(2,1)S(1)} %convert_element_type.58), channel_id=1, source_target_pairs={{0,1},{1,0},{2,3},{3,2},{4,5},{5,4},{6,7},{7,6},{8,9},{9,8},{10,11... | collective-permute-start | bytes 786440 | tf_op jit(solution)/shard_map/ppermute | solution.py:108
  69.5 9.0 %collective-permute-done.11 = f16[256,1024]{1,0:T(8,128)(2,1)S(1)} collective-permute-done((f16[256,1024]{1,0:T(8,128)(2,1)S(1)}, f16[256,1024]{1,0:T(8,128)(2,1)S(1)}, u32[]{:S(2)}, u32[]{:S(2)}) %collective-permute-start.11) | collective-permute-done | bytes 524320 | tf_op jit(solution)/shard_map/ppermute | solution.py:108
  78.7 11.0 %collective-permute-done.10 = f16[256,1024]{1,0:T(8,128)(2,1)S(1)} collective-permute-done((f16[256,1024]{1,0:T(8,128)(2,1)S(1)}, f16[256,1024]{1,0:T(8,128)(2,1)S(1)}, u32[]{:S(2)}, u32[]{:S(2)}) %collective-permute-start.10) | collective-permute-done | bytes 524320 | tf_op jit(solution)/shard_map/ppermute | solution.py:108
  89.9 2.1 %shard_map.105 = (f32[8,256]{1,0:T(8,128)S(1)}, f32[1792,256]{1,0:T(8,128)S(1)}) custom-call(f32[256,1024]{1,0:T(8,128)S(1)} %get-tuple-element.105.logits_ref, s32[256,1]{1,0:T(8,128)S(1)} %get-tuple-element.55.target_ref, bf16[1792,5120]{1,0:T(8,128)(2,1)S(1)} %shard_map.94.weight_ref, ...), custom_call_target="tpu_custom_call", output_to_operand_aliasing={{1}: (4, {})} | custom-call | flops 939524096 | bytes 8388608 | tf_op jit(solution)/shard_map/pallas_call | solution.py:190
  92.1 2.1 %shard_map.106 = (f32[8,256]{1,0:T(8,128)S(1)}, f32[1792,256]{1,0:T(8,128)S(1)}) custom-call(f32[256,1024]{1,0:T(8,128)S(1)} %get-tuple-element.103.logits_ref, s32[256,1]{1,0:T(8,128)S(1)} %get-tuple-element.55.target_ref, bf16[1792,5120]{1,0:T(8,128)(2,1)S(1)} %shard_map.94.weight_ref, ...), custom_call_target="tpu_custom_call", output_to_operand_aliasing={{1}: (4, {})} | custom-call | flops 939524096 | bytes 8388608 | tf_op jit(solution)/shard_map/pallas_call | solution.py:190
  94.2 2.1 %shard_map.107 = (f32[8,256]{1,0:T(8,128)S(1)}, f32[1792,256]{1,0:T(8,128)S(1)}) custom-call(f32[256,1024]{1,0:T(8,128)S(1)} %get-tuple-element.101.logits_ref, s32[256,1]{1,0:T(8,128)S(1)} %get-tuple-element.55.target_ref, bf16[1792,5120]{1,0:T(8,128)(2,1)S(1)} %shard_map.94.weight_ref, ...), custom_call_target="tpu_custom_call", output_to_operand_aliasing={{1}: (4, {})} | custom-call | flops 939524096 | bytes 8388608 | tf_op jit(solution)/shard_map/pallas_call | solution.py:190
  97.9 2.8 %collective-permute-done.7 = f16[256,512]{1,0:T(8,128)(2,1)S(1)} collective-permute-done((f16[256,512]{1,0:T(8,128)(2,1)S(1)}, f16[256,512]{1,0:T(8,128)(2,1)S(1)}, u32[]{:S(2)}, u32[]{:S(2)}) %collective-permute-start.7) | collective-permute-done | bytes 262176 | tf_op jit(solution)/shard_map/ppermute | solution.py:108
  106.5 5.7 %collective-permute-done.21.got_ref = bf16[448,256]{1,0:T(8,128)(2,1)S(1)} collective-permute-done((bf16[448,256]{1,0:T(8,128)(2,1)S(1)}, bf16[448,256]{1,0:T(8,128)(2,1)S(1)}, u32[]{:S(2)}, u32[]{:S(2)}) %collective-permute-start.21) | collective-permute-done | bytes 229408 | tf_op jit(solution)/shard_map/ppermute | solution.py:104
  112.9 3.9 %collective-permute-done.16.got_ref = bf16[464,256]{1,0:T(8,128)(2,1)S(1)} collective-permute-done((bf16[464,256]{1,0:T(8,128)(2,1)S(1)}, bf16[464,256]{1,0:T(8,128)(2,1)S(1)}, u32[]{:S(2)}, u32[]{:S(2)}) %collective-permute-start.16) | collective-permute-done | bytes 237600 | tf_op jit(solution)/shard_map/ppermute | solution.py:104
  119.4 2.5 %collective-permute-start.19 = (bf16[256,128]{1,0:T(8,128)(2,1)S(1)}, bf16[256,128]{1,0:T(8,128)(2,1)S(1)}, u32[]{:S(2)}, u32[]{:S(2)}) collective-permute-start(bf16[256,128]{1,0:T(8,128)(2,1)S(1)} %get-tuple-element.78), channel_id=1, source_target_pairs={{0,24},{2,26},{4,28},{6,30},{8,16},{10,18},{12,20},{14,22},{16,8},... | collective-permute-start | bytes 196616 | tf_op jit(solution)/shard_map/ppermute | solution.py:104
  123.5 7.2 %collective-permute-done.23.picked_c_ref = bf16[224,128]{1,0:T(8,128)(2,1)S(1)} collective-permute-done((bf16[224,128]{1,0:T(8,128)(2,1)S(1)}, bf16[224,128]{1,0:T(8,128)(2,1)S(1)}, u32[]{:S(2)}, u32[]{:S(2)}) %collective-permute-start.23) | collective-permute-done | bytes 57376 | tf_op jit(solution)/shard_map/ppermute | solution.py:104
  132.3 4.3 %collective-permute-start.25 = (f32[16,128]{1,0:T(8,128)S(1)}, f32[16,128]{1,0:T(8,128)S(1)}, u32[]{:S(2)}, u32[]{:S(2)}) collective-permute-start(f32[16,128]{1,0:T(8,128)S(1)} %get-tuple-element.89.rows_ref), channel_id=1, source_target_pairs={{0,1},{1,0},{2,3},{3,2},{4,5},{5,4},{6,7},{7,6},{8,9},{9,8},{10,11... | collective-permute-start | bytes 24584 | tf_op jit(solution)/shard_map/ppermute | solution.py:108
  136.6 9.9 %shard_map.118 = bf16[1792,5120]{1,0:T(8,128)(2,1)} custom-call(bf16[1792,256]{1,0:T(8,128)(2,1)S(1)} %get-tuple-element.94.hidden_ref, f32[256,5120]{1,0:T(8,128)S(1)} %get-tuple-element.96.logits_ref, f32[256,8]{1,0:T(8,128)S(1)} %get-tuple-element.95.rows_ref, s32[256,1]{1,0:T(8,128)S(1)} %get-tuple-element.55.target_ref), custom_call_target="tpu_custom_call" | custom-call | flops 4697620480 | bytes 23592960 | tf_op jit(solution)/shard_map/pallas_call | solution.py:627
  (79 shorter events, 34.8 us)
Async XLA Ops:
  4.4 11.5 %collective-permute-start.1 = (bf16[224,128]{1,0:T(8,128)(2,1)S(1)}, bf16[224,128]{1,0:T(8,128)(2,1)S(1)}, u32[]{:S(2)}, u32[]{:S(2)}) collective-permute-start(bf16[224,128]{1,0:T(8,128)(2,1)S(1)} %broadcast_select_fusion), channel_id=1, source_target_pairs={{0,8},{2,10},{4,12},{6,14},{8,0},{10,2},{12,4},{14,6},{16,24},{18,... | collective-permute-start | bytes 172040 | tf_op jit(solution)/shard_map/ppermute | solution.py:104
  7.4 11.8 %collective-permute-start.2 = (bf16[224,128]{1,0:T(8,128)(2,1)S(1)}, bf16[224,128]{1,0:T(8,128)(2,1)S(1)}, u32[]{:S(2)}, u32[]{:S(2)}) collective-permute-start(bf16[224,128]{1,0:T(8,128)(2,1)S(1)} %broadcast_select_fusion), channel_id=1, source_target_pairs={{0,16},{2,18},{4,20},{6,22},{8,24},{10,26},{12,28},{14,30},{16,0},... | collective-permute-start | bytes 172040 | tf_op jit(solution)/shard_map/ppermute | solution.py:104
  21.8 8.7 %collective-permute-start.4 = (bf16[896,128]{1,0:T(8,128)(2,1)S(1)}, bf16[896,128]{1,0:T(8,128)(2,1)S(1)}, u32[]{:S(2)}, u32[]{:S(2)}) collective-permute-start(bf16[896,128]{1,0:T(8,128)(2,1)S(1)} %pad_maximum_fusion), channel_id=1, source_target_pairs={{0,4},{2,6},{4,0},{6,2},{8,12},{10,14},{12,8},{14,10},{16,20},{18,... | collective-permute-start | bytes 688136 | tf_op jit(solution)/shard_map/ppermute | solution.py:104
  23.4 6.4 %collective-permute-start.8 = (f32[8,128]{1,0:T(8,128)S(1)}, f32[8,128]{1,0:T(8,128)S(1)}, u32[]{:S(2)}, u32[]{:S(2)}) collective-permute-start(f32[8,128]{1,0:T(8,128)S(1)} %concatenate.9.own_ref), channel_id=1, source_target_pairs={{0,1},{1,0},{2,3},{3,2},{4,5},{5,4},{6,7},{7,6},{8,9},{9,8},{10,11... | collective-permute-start | bytes 12296 | tf_op jit(solution)/shard_map/ppermute | solution.py:108
  30.5 7.1 %collective-permute-start.5 = (bf16[896,128]{1,0:T(8,128)(2,1)S(1)}, bf16[896,128]{1,0:T(8,128)(2,1)S(1)}, u32[]{:S(2)}, u32[]{:S(2)}) collective-permute-start(bf16[896,128]{1,0:T(8,128)(2,1)S(1)} %pad_maximum_fusion), channel_id=1, source_target_pairs={{0,2},{2,0},{4,6},{6,4},{8,10},{10,8},{12,14},{14,12},{16,18},{18,... | collective-permute-start | bytes 688136 | tf_op jit(solution)/shard_map/ppermute | solution.py:104
  30.6 7.1 %collective-permute-start.6 = (bf16[896,128]{1,0:T(8,128)(2,1)S(1)}, bf16[896,128]{1,0:T(8,128)(2,1)S(1)}, u32[]{:S(2)}, u32[]{:S(2)}) collective-permute-start(bf16[896,128]{1,0:T(8,128)(2,1)S(1)} %collective-permute-done.4), channel_id=1, source_target_pairs={{0,2},{2,0},{4,6},{6,4},{8,10},{10,8},{12,14},{14,12},{16,18},{18,... | collective-permute-start | bytes 688136 | tf_op jit(solution)/shard_map/ppermute | solution.py:104
  37.5 65.5 %collective-permute-start.20 = (bf16[896,256]{1,0:T(8,128)(2,1)S(1)}, bf16[896,256]{1,0:T(8,128)(2,1)S(1)}, u32[]{:S(2)}, u32[]{:S(2)}) collective-permute-start(bf16[896,256]{1,0:T(8,128)(2,1)S(1)} %get-tuple-element.81), channel_id=1, source_target_pairs={{0,2},{2,0},{4,6},{6,4},{8,10},{10,8},{12,14},{14,12},{16,18},{18,... | collective-permute-start | bytes 1376264 | tf_op jit(solution)/shard_map/ppermute | solution.py:104
  41.1 9.2 %collective-permute-start.14 = (f16[256,512]{1,0:T(8,128)(2,1)S(1)}, f16[256,512]{1,0:T(8,128)(2,1)S(1)}, u32[]{:S(2)}, u32[]{:S(2)}) collective-permute-start(f16[256,512]{1,0:T(8,128)(2,1)S(1)} %convert_element_type.70), channel_id=1, source_target_pairs={{0,1},{1,0},{2,3},{3,2},{4,5},{5,4},{6,7},{7,6},{8,9},{9,8},{10,11... | collective-permute-start | bytes 786440 | tf_op jit(solution)/shard_map/ppermute | solution.py:108
  43.3 12.7 %collective-permute-start.13 = (f16[256,512]{1,0:T(8,128)(2,1)S(1)}, f16[256,512]{1,0:T(8,128)(2,1)S(1)}, u32[]{:S(2)}, u32[]{:S(2)}) collective-permute-start(f16[256,512]{1,0:T(8,128)(2,1)S(1)} %convert_element_type.68), channel_id=1, source_target_pairs={{0,1},{1,0},{2,3},{3,2},{4,5},{5,4},{6,7},{7,6},{8,9},{9,8},{10,11... | collective-permute-start | bytes 786440 | tf_op jit(solution)/shard_map/ppermute | solution.py:108
  43.4 23.8 %collective-permute-start.12 = (f16[256,1024]{1,0:T(8,128)(2,1)S(1)}, f16[256,1024]{1,0:T(8,128)(2,1)S(1)}, u32[]{:S(2)}, u32[]{:S(2)}) collective-permute-start(f16[256,1024]{1,0:T(8,128)(2,1)S(1)} %convert_element_type.66), channel_id=1, source_target_pairs={{0,1},{1,0},{2,3},{3,2},{4,5},{5,4},{6,7},{7,6},{8,9},{9,8},{10,11... | collective-permute-start | bytes 1572872 | tf_op jit(solution)/shard_map/ppermute | solution.py:108
  46.7 31.7 %collective-permute-start.11 = (f16[256,1024]{1,0:T(8,128)(2,1)S(1)}, f16[256,1024]{1,0:T(8,128)(2,1)S(1)}, u32[]{:S(2)}, u32[]{:S(2)}) collective-permute-start(f16[256,1024]{1,0:T(8,128)(2,1)S(1)} %convert_element_type.64), channel_id=1, source_target_pairs={{0,1},{1,0},{2,3},{3,2},{4,5},{5,4},{6,7},{7,6},{8,9},{9,8},{10,11... | collective-permute-start | bytes 1572872 | tf_op jit(solution)/shard_map/ppermute | solution.py:108
  50.4 39.3 %collective-permute-start.10 = (f16[256,1024]{1,0:T(8,128)(2,1)S(1)}, f16[256,1024]{1,0:T(8,128)(2,1)S(1)}, u32[]{:S(2)}, u32[]{:S(2)}) collective-permute-start(f16[256,1024]{1,0:T(8,128)(2,1)S(1)} %convert_element_type.62), channel_id=1, source_target_pairs={{0,1},{1,0},{2,3},{3,2},{4,5},{5,4},{6,7},{7,6},{8,9},{9,8},{10,11... | collective-permute-start | bytes 1572872 | tf_op jit(solution)/shard_map/ppermute | solution.py:108
  56.0 40.3 %collective-permute-start.9 = (f16[256,512]{1,0:T(8,128)(2,1)S(1)}, f16[256,512]{1,0:T(8,128)(2,1)S(1)}, u32[]{:S(2)}, u32[]{:S(2)}) collective-permute-start(f16[256,512]{1,0:T(8,128)(2,1)S(1)} %convert_element_type.60), channel_id=1, source_target_pairs={{0,1},{1,0},{2,3},{3,2},{4,5},{5,4},{6,7},{7,6},{8,9},{9,8},{10,11... | collective-permute-start | bytes 786440 | tf_op jit(solution)/shard_map/ppermute | solution.py:108
  67.2 33.5 %collective-permute-start.7 = (f16[256,512]{1,0:T(8,128)(2,1)S(1)}, f16[256,512]{1,0:T(8,128)(2,1)S(1)}, u32[]{:S(2)}, u32[]{:S(2)}) collective-permute-start(f16[256,512]{1,0:T(8,128)(2,1)S(1)} %convert_element_type.58), channel_id=1, source_target_pairs={{0,1},{1,0},{2,3},{3,2},{4,5},{5,4},{6,7},{7,6},{8,9},{9,8},{10,11... | collective-permute-start | bytes 786440 | tf_op jit(solution)/shard_map/ppermute | solution.py:108
  103.6 8.5 %collective-permute-start.21 = (bf16[448,256]{1,0:T(8,128)(2,1)S(1)}, bf16[448,256]{1,0:T(8,128)(2,1)S(1)}, u32[]{:S(2)}, u32[]{:S(2)}) collective-permute-start(bf16[448,256]{1,0:T(8,128)(2,1)S(1)} %get-tuple-element.83), channel_id=1, source_target_pairs={{0,4},{2,6},{4,0},{6,2},{8,12},{10,14},{12,8},{14,10},{16,20},{18,... | collective-permute-start | bytes 688136 | tf_op jit(solution)/shard_map/ppermute | solution.py:104
  105.5 11.3 %collective-permute-start.16 = (bf16[464,256]{1,0:T(8,128)(2,1)S(1)}, bf16[464,256]{1,0:T(8,128)(2,1)S(1)}, u32[]{:S(2)}, u32[]{:S(2)}) collective-permute-start(bf16[464,256]{1,0:T(8,128)(2,1)S(1)} %get-tuple-element.73), channel_id=1, source_target_pairs={{0,4},{2,6},{4,0},{6,2},{8,12},{10,14},{12,8},{14,10},{16,20},{18,... | collective-permute-start | bytes 712712 | tf_op jit(solution)/shard_map/ppermute | solution.py:104
  112.8 9.1 %collective-permute-start.22 = (bf16[224,128]{1,0:T(8,128)(2,1)S(1)}, bf16[224,128]{1,0:T(8,128)(2,1)S(1)}, u32[]{:S(2)}, u32[]{:S(2)}) collective-permute-start(bf16[224,128]{1,0:T(8,128)(2,1)S(1)} %get-tuple-element.85), channel_id=1, source_target_pairs={{0,8},{2,10},{4,12},{6,14},{8,0},{10,2},{12,4},{14,6},{16,24},{18,... | collective-permute-start | bytes 172040 | tf_op jit(solution)/shard_map/ppermute | solution.py:104
  117.5 13.2 %collective-permute-start.17 = (bf16[256,128]{1,0:T(8,128)(2,1)S(1)}, bf16[256,128]{1,0:T(8,128)(2,1)S(1)}, u32[]{:S(2)}, u32[]{:S(2)}) collective-permute-start(bf16[256,128]{1,0:T(8,128)(2,1)S(1)} %get-tuple-element.76), channel_id=1, source_target_pairs={{0,8},{2,10},{4,12},{6,14},{8,0},{10,2},{12,4},{14,6},{16,24},{18,... | collective-permute-start | bytes 196616 | tf_op jit(solution)/shard_map/ppermute | solution.py:104
  117.6 13.1 %collective-permute-start.18 = (bf16[256,128]{1,0:T(8,128)(2,1)S(1)}, bf16[256,128]{1,0:T(8,128)(2,1)S(1)}, u32[]{:S(2)}, u32[]{:S(2)}) collective-permute-start(bf16[256,128]{1,0:T(8,128)(2,1)S(1)} %get-tuple-element.77), channel_id=1, source_target_pairs={{0,16},{2,18},{4,20},{6,22},{8,24},{10,26},{12,28},{14,30},{16,0},... | collective-permute-start | bytes 196616 | tf_op jit(solution)/shard_map/ppermute | solution.py:104
  119.4 11.3 %collective-permute-start.19 = (bf16[256,128]{1,0:T(8,128)(2,1)S(1)}, bf16[256,128]{1,0:T(8,128)(2,1)S(1)}, u32[]{:S(2)}, u32[]{:S(2)}) collective-permute-start(bf16[256,128]{1,0:T(8,128)(2,1)S(1)} %get-tuple-element.78), channel_id=1, source_target_pairs={{0,24},{2,26},{4,28},{6,30},{8,16},{10,18},{12,20},{14,22},{16,8},... | collective-permute-start | bytes 196616 | tf_op jit(solution)/shard_map/ppermute | solution.py:104
  122.0 8.7 %collective-permute-start.23 = (bf16[224,128]{1,0:T(8,128)(2,1)S(1)}, bf16[224,128]{1,0:T(8,128)(2,1)S(1)}, u32[]{:S(2)}, u32[]{:S(2)}) collective-permute-start(bf16[224,128]{1,0:T(8,128)(2,1)S(1)} %get-tuple-element.86), channel_id=1, source_target_pairs={{0,16},{2,18},{4,20},{6,22},{8,24},{10,26},{12,28},{14,30},{16,0},... | collective-permute-start | bytes 172040 | tf_op jit(solution)/shard_map/ppermute | solution.py:104
  122.0 8.7 %collective-permute-start.24 = (bf16[224,128]{1,0:T(8,128)(2,1)S(1)}, bf16[224,128]{1,0:T(8,128)(2,1)S(1)}, u32[]{:S(2)}, u32[]{:S(2)}) collective-permute-start(bf16[224,128]{1,0:T(8,128)(2,1)S(1)} %get-tuple-element.87), channel_id=1, source_target_pairs={{0,24},{2,26},{4,28},{6,30},{8,16},{10,18},{12,20},{14,22},{16,8},... | collective-permute-start | bytes 172040 | tf_op jit(solution)/shard_map/ppermute | solution.py:104
  131.6 14.9 %collective-permute-start.26 = (bf16[224,128]{1,0:T(8,128)(2,1)S(1)}, bf16[224,128]{1,0:T(8,128)(2,1)S(1)}, u32[]{:S(2)}, u32[]{:S(2)}) collective-permute-start(bf16[224,128]{1,0:T(8,128)(2,1)S(1)} %get-tuple-element.90.own_ref), channel_id=1, source_target_pairs={{16,1},{18,3},{20,5},{22,7},{24,9},{26,11},{28,13},{30,15},{1,16},... | collective-permute-start | bytes 172040 | tf_op jit(solution)/shard_map/ppermute | solution.py:118
  132.3 14.3 %collective-permute-start.25 = (f32[16,128]{1,0:T(8,128)S(1)}, f32[16,128]{1,0:T(8,128)S(1)}, u32[]{:S(2)}, u32[]{:S(2)}) collective-permute-start(f32[16,128]{1,0:T(8,128)S(1)} %get-tuple-element.89.rows_ref), channel_id=1, source_target_pairs={{0,1},{1,0},{2,3},{3,2},{4,5},{5,4},{6,7},{7,6},{8,9},{9,8},{10,11... | collective-permute-start | bytes 24584 | tf_op jit(solution)/shard_map/ppermute | solution.py:108
  (3 other events, 10.8 us)

commit v3 on v2

--- a/solution.py
+++ b/solution.py
@@ -91,7 +91,7 @@
 hidden_bound = 8.0
 weight_bound = 4.0
 half_limit = 60000.0
-part_tiles = (4, 4, 8, 8, 8, 4, 4)
+part_tiles = (2, 4, 8, 8, 8, 6, 2, 2)
 mebi = 1 << 20
 stats_rows = 16
 
@@ -136,7 +136,7 @@
         hidden_n_ref[:, start : start + step] = hidden_t_ref[start : start + step, :].T
 
 
-def fold_kernel(start, has_state, logits_ref, target_ref, weight_ref, *refs):
+def fold_kernel(start, has_state, logits_ref, target_ref, upper_ref, lower_ref, *refs):
     if has_state:
         stats_ref, grad_ref, new_stats_ref, new_grad_ref, terms_ref = refs
     else:
@@ -165,11 +165,10 @@
     ).T
     new_stats_ref[...] = packed[0:8]
     shrink_row = packed[3:4]
-    depth = weight_ref.shape[0]
-    step = depth // 2 if depth % 256 == 0 else depth
-    for first in range(0, depth, step):
+    step = upper_ref.shape[0]
+    for first, weight_ref in ((0, upper_ref), (step, lower_ref)):
         part = lax.dot_general(
-            weight_ref[first : first + step, start : start + width],
+            weight_ref[:, start : start + width],
             terms_ref[...],
             (((1,), (1,)), ((), ())),
             preferred_element_type=jnp.float32,
@@ -181,12 +180,12 @@
 
 def fold(start, width, logits, local_targets, head_weight, state):
     tokens = logits.shape[0]
-    depth = head_weight.shape[0]
-    args = [logits, local_targets, head_weight]
+    depth = 2 * head_weight[0].shape[0]
+    args = [logits, local_targets, *head_weight]
     aliases = {}
     if state is not None:
         args += list(state)
-        aliases = {4: 1}
+        aliases = {5: 1}
     return pl.pallas_call(
         functools.partial(fold_kernel, start, state is not None),
         out_shape=(
@@ -206,12 +205,12 @@
     )(*args)
 
 
-def load_kernel(source_ref, held_ref, sems):
+def load_kernel(first, source_ref, held_ref, sems):
     number = sems.shape[0]
-    rows = source_ref.shape[0] // number
+    rows = held_ref.shape[0] // number
     copies = [
         pltpu.make_async_copy(
-            source_ref.at[pl.ds(index * rows, rows)],
+            source_ref.at[pl.ds(first + index * rows, rows)],
             held_ref.at[pl.ds(index * rows, rows)],
             sems.at[index],
         )
@@ -223,29 +222,32 @@
         copy.wait()
 
 
-def load(head_weight):
-    depth = head_weight.shape[0]
-    number = 8 if depth % 256 == 0 else 1
+def load(head_weight, first, rows, limit):
+    cols = head_weight.shape[1]
+    number = 4 if rows % 64 == 0 else 1
     return pl.pallas_call(
-        load_kernel,
-        out_shape=pltpu.VMEM(head_weight.shape, head_weight.dtype),
+        functools.partial(load_kernel, first),
+        out_shape=pltpu.VMEM((rows, cols), head_weight.dtype),
         in_specs=[pl.BlockSpec(memory_space=pl.ANY)],
         out_specs=pl.BlockSpec(memory_space=pltpu.VMEM),
         scratch_shapes=[pltpu.SemaphoreType.DMA((number,))],
-        compiler_params=pltpu.CompilerParams(vmem_limit_bytes=20 * mebi),
-        cost_estimate=pl.CostEstimate(
-            flops=0, transcendentals=0, bytes_accessed=2 * head_weight.size
-        ),
+        compiler_params=pltpu.CompilerParams(vmem_limit_bytes=limit * mebi),
+        cost_estimate=pl.CostEstimate(flops=0, transcendentals=0, bytes_accessed=2 * rows * cols),
     )(head_weight)
 
 
-def logit_kernel(start, hidden_ref, weight_ref, out_ref):
+def logit_kernel(start, hidden_ref, upper_ref, lower_ref, out_ref):
     width = out_ref.shape[1]
+    half = upper_ref.shape[0]
     step = 256 if width % 256 == 0 else width
     for first in range(0, width, step):
         out_ref[:, first : first + step] = jnp.dot(
-            hidden_ref[...],
-            weight_ref[:, start + first : start + first + step],
+            hidden_ref[:, :half],
+            upper_ref[:, start + first : start + first + step],
+            preferred_element_type=jnp.float32,
+        ) + jnp.dot(
+            hidden_ref[:, half:],
+            lower_ref[:, start + first : start + first + step],
             preferred_element_type=jnp.float32,
         )
 
@@ -255,13 +257,13 @@
     return pl.pallas_call(
         functools.partial(logit_kernel, start),
         out_shape=jax.ShapeDtypeStruct((tokens, width), jnp.float32),
-        in_specs=vmem_specs(2),
+        in_specs=vmem_specs(3),
         out_specs=vmem_specs(1)[0],
         compiler_params=pltpu.CompilerParams(vmem_limit_bytes=12 * mebi),
         cost_estimate=pl.CostEstimate(
             flops=2 * depth * tokens * width, transcendentals=0, bytes_accessed=2 * depth * width
         ),
-    )(hidden_n, head_weight)
+    )(hidden_n, *head_weight)
 
 
 def gather_hidden(piece, where, count):
@@ -293,22 +295,24 @@
     )
 
 
-def pick_kernel(feats, spot_ref, target_ref, weight_ref, keep_ref, send_ref, sum_ref):
-    _, cols = weight_ref.shape
+def pick_kernel(feats, spot_ref, target_ref, upper_ref, lower_ref, keep_ref, send_ref, sum_ref):
+    half, cols = upper_ref.shape
     width = 1024 if cols % 1024 == 0 else cols
     columns = lax.broadcasted_iota(jnp.int32, (target_ref.shape[0], width), 1)
     for start in range(0, cols, width):
         hit = columns + start == target_ref[...]
-        part = lax.dot_general(
-            weight_ref[:, start : start + width],
-            jnp.where(hit, 1.0, 0.0).astype(jnp.bfloat16),
-            (((1,), (1,)), ((), ())),
-            preferred_element_type=jnp.float32,
-        )
-        if start == 0:
-            sum_ref[...] = part
-        else:
-            sum_ref[...] += part
+        ones = jnp.where(hit, 1.0, 0.0).astype(jnp.bfloat16)
+        for first, weight_ref in ((0, upper_ref), (half, lower_ref)):
+            part = lax.dot_general(
+                weight_ref[:, start : start + width],
+                ones,
+                (((1,), (1,)), ((), ())),
+                preferred_element_type=jnp.float32,
+            )
+            if start == 0:
+                sum_ref[first : first + half, :] = part
+            else:
+                sum_ref[first : first + half, :] += part
     bit = spot_ref[0] % 2
     for group in range(keep_ref.shape[0] // feats):
         out = pl.ds(group * feats, feats)
@@ -343,14 +347,14 @@
 
 def pick(where, local_targets, head_weight, count):
     tokens = local_targets.shape[0]
-    depth, cols = head_weight.shape
+    depth, cols = 2 * head_weight[0].shape[0], head_weight[0].shape[1]
     feats = 2 * depth // count
     rows = tokens // 2
     bf16 = jnp.bfloat16
     keep, send = pl.pallas_call(
         functools.partial(pick_kernel, feats),
         out_shape=[jax.ShapeDtypeStruct((depth // 2, tokens), bf16)] * 2,
-        in_specs=[pl.BlockSpec(memory_space=pltpu.SMEM)] + vmem_specs(2),
+        in_specs=[pl.BlockSpec(memory_space=pltpu.SMEM)] + vmem_specs(3),
         out_specs=vmem_specs(2),
         scratch_shapes=[pltpu.VMEM((depth, tokens), jnp.float32)],
         compiler_params=pltpu.CompilerParams(vmem_limit_bytes=14 * mebi),
@@ -359,7 +363,7 @@
             transcendentals=0,
             bytes_accessed=2 * depth * cols,
         ),
-    )(where, local_targets, head_weight)
+    )(where, local_targets, *head_weight)
     got = across(send, count, 1)
     keep, send = small_call(
         functools.partial(pick_next_kernel, feats),
@@ -621,7 +625,7 @@
 def head_blocks(hidden_t, logits, row_values, local_targets):
     depth, tokens = hidden_t.shape
     cols = logits.shape[1]
-    width = cols // 5 if cols % (5 * 256) == 0 else cols
+    width = cols // 4 if cols % (4 * 256) == 0 else cols
     whole = lambda step: (0, 0)
     column = lambda step: (0, step)
     return pl.pallas_call(
@@ -702,7 +706,9 @@
     )
     where, moves, info, head_weight = lax.optimization_barrier((where, moves, info, head_weight))
     piece = plane_swap(hidden.T, count, moves)
-    head_weight = load(head_weight)
+    upper = load(head_weight, 0, depth // 2, 48)
+    lower = load(head_weight, depth // 2, depth // 2, 40)
+    head_weight = (upper, lower)
     hidden_t, hidden_n = gather_hidden(piece, where, count)
     rows_info, local_targets = small_call(
         functools.partial(side_kernel, cols),

time: 148 us -> 153 us (1.034)
  starting transfers between devices: 37.4 us -> 39.6 us
  waiting for transfers between devices: 57.3 us -> 59.1 us
    ppermute x9 -> x10, starting transfers between devices: 14.7 us -> 16.8 us  [over(): return lax.ppermute(value, 'tok', swap_pairs)]
    ppermute x9 -> x10, waiting for transfers between devices: 33.9 us -> 35.8 us  [over(): return lax.ppermute(value, 'tok', swap_pairs)]
    pallas_call x1 -> x2, Pallas kernels: 6.37 us -> 7.45 us  [load(): pl.pallas_call(functools.partial(load_kernel, first), out_shape=pltpu.VME...]
    pallas_call x7 -> x8, Pallas kernels: 6 us -> 6.66 us  [logit_part(): pl.pallas_call(functools.partial(logit_kernel, start), out_shape=jax.Shap...]
    pallas_call x7 -> x8, Pallas kernels: 11.8 us -> 12.1 us  [fold(): pl.pallas_call(functools.partial(fold_kernel, start, state is not None),...]
  transfers between devices with their start and end apart: 27 -> 28, of which waited for: 12 -> 11; matrix products, arithmetic and copies ran while one was open for 2% -> 2% of each run, Pallas kernels for 31% -> 30%
where the time goes in v3:
time: 153 us
  waiting for transfers between devices  59.1 us (39%)
  Pallas kernels  48.5 us (32%)
  starting transfers between devices  39.6 us (26%)
  other arithmetic  3.25 us (2%)
  between operations  1.76 us (1%)
    ppermute x10, waiting for transfers between devices, over(): return lax.ppermute(value, 'tok', swap_pairs)  35.8 us
    ppermute x16, waiting for transfers between devices, across(): return lax.ppermute(value, 'vocab', exclusive(count, mask))  23.3 us
    ppermute x16, starting transfers between devices, across(): return lax.ppermute(value, 'vocab', exclusive(count, mask))  21.4 us
    ppermute x10, starting transfers between devices, over(): return lax.ppermute(value, 'tok', swap_pairs)  16.8 us
    pallas_call x8, Pallas kernels, fold(): pl.pallas_call(functools.partial(fold_kernel, start, state is not None),...  12.1 us
    pallas_call x1, Pallas kernels, head_blocks(): pl.pallas_call(head_kernel, out_shape=jax.ShapeDtypeStruct((depth, cols),...  9.44 us
    pallas_call x2, Pallas kernels, load(): pl.pallas_call(functools.partial(load_kernel, first), out_shape=pltpu.VME...  7.45 us
    pallas_call x8, Pallas kernels, logit_part(): pl.pallas_call(functools.partial(logit_kernel, start), out_shape=jax.Shap...  6.66 us
  transfers between devices with their start and end apart: 28, of which 11 were waited for; matrix products, arithmetic and copies ran while one was open for 2% of the time, Pallas kernels for 30%

profile of v3, /device:TPU:0, one launch (start us, length us, event | category | flops | bytes accessed | tf_op | source)
XLA Modules:
  0.0 153.0 jit_solution(3575139424454347041)
XLA Ops:
  4.4 3.1 %collective-permute-start.1 = (bf16[224,128]{1,0:T(8,128)(2,1)S(1)}, bf16[224,128]{1,0:T(8,128)(2,1)S(1)}, u32[]{:S(2)}, u32[]{:S(2)}) collective-permute-start(bf16[224,128]{1,0:T(8,128)(2,1)S(1)} %broadcast_select_fusion), channel_id=1, source_target_pairs={{0,8},{2,10},{4,12},{6,14},{8,0},{10,2},{12,4},{14,6},{16,24},{18,... | collective-permute-start | bytes 172040 | tf_op jit(solution)/shard_map/ppermute | solution.py:104
  7.4 8.4 %collective-permute-start.2 = (bf16[224,128]{1,0:T(8,128)(2,1)S(1)}, bf16[224,128]{1,0:T(8,128)(2,1)S(1)}, u32[]{:S(2)}, u32[]{:S(2)}) collective-permute-start(bf16[224,128]{1,0:T(8,128)(2,1)S(1)} %broadcast_select_fusion), channel_id=1, source_target_pairs={{0,16},{2,18},{4,20},{6,22},{8,24},{10,26},{12,28},{14,30},{16,0},... | collective-permute-start | bytes 172040 | tf_op jit(solution)/shard_map/ppermute | solution.py:104
  15.8 3.4 %collective-permute-done.2 = bf16[224,128]{1,0:T(8,128)(2,1)S(1)} collective-permute-done((bf16[224,128]{1,0:T(8,128)(2,1)S(1)}, bf16[224,128]{1,0:T(8,128)(2,1)S(1)}, u32[]{:S(2)}, u32[]{:S(2)}) %collective-permute-start.2) | collective-permute-done | bytes 57376 | tf_op jit(solution)/shard_map/ppermute | solution.py:104
  19.2 2.6 %collective-permute-done.3 = bf16[224,128]{1,0:T(8,128)(2,1)S(1)} collective-permute-done((bf16[224,128]{1,0:T(8,128)(2,1)S(1)}, bf16[224,128]{1,0:T(8,128)(2,1)S(1)}, u32[]{:S(2)}, u32[]{:S(2)}) %collective-permute-start.3) | collective-permute-done | bytes 57376 | tf_op jit(solution)/shard_map/ppermute | solution.py:104
  23.4 3.7 %shard_map.94.upper_ref = bf16[896,5120]{1,0:T(8,128)(2,1)S(1)} custom-call(bf16[1792,5120]{1,0:T(8,128)(2,1)} %source_ref.1), custom_call_target="tpu_custom_call" | custom-call | bytes 9175040 | tf_op jit(solution)/shard_map/pallas_call | solution.py:228
  27.1 3.7 %shard_map.95.lower_ref = bf16[896,5120]{1,0:T(8,128)(2,1)S(1)} custom-call(bf16[1792,5120]{1,0:T(8,128)(2,1)} %source_ref.1), custom_call_target="tpu_custom_call" | custom-call | bytes 9175040 | tf_op jit(solution)/shard_map/pallas_call | solution.py:228
  32.2 5.7 %shard_map.116 = (bf16[896,256]{1,0:T(8,128)(2,1)S(1)}, bf16[896,256]{1,0:T(8,128)(2,1)S(1)}) custom-call(s32[3]{0:T(128)S(1)} %pad_add_fusion.refs_0_.place_ref.spot_ref, s32[256,1]{1,0:T(8,128)S(1)} %get-tuple-element.57.target_ref, bf16[896,5120]{1,0:T(8,128)(2,1)S(1)} %shard_map.94.upper_ref, bf16[896,5120]{1,0:T(8,128)(2,1)S(1)} %shard_map.95.lower_ref), custom_call_target="tpu_custom_call" | custom-call | flops 4697620480 | bytes 18350080 | tf_op jit(solution)/shard_map/pallas_call | solution.py:354
  43.2 2.1 %collective-permute-start.15 = (f16[256,256]{1,0:T(8,128)(2,1)S(1)}, f16[256,256]{1,0:T(8,128)(2,1)S(1)}, u32[]{:S(2)}, u32[]{:S(2)}) collective-permute-start(f16[256,256]{1,0:T(8,128)(2,1)S(1)} %convert_element_type.78), channel_id=1, source_target_pairs={{0,1},{1,0},{2,3},{3,2},{4,5},{5,4},{6,7},{7,6},{8,9},{9,8},{10,11... | collective-permute-start | bytes 393224 | tf_op jit(solution)/shard_map/ppermute | solution.py:108
  46.2 2.1 %collective-permute-start.13 = (f16[256,1024]{1,0:T(8,128)(2,1)S(1)}, f16[256,1024]{1,0:T(8,128)(2,1)S(1)}, u32[]{:S(2)}, u32[]{:S(2)}) collective-permute-start(f16[256,1024]{1,0:T(8,128)(2,1)S(1)} %convert_element_type.74), channel_id=1, source_target_pairs={{0,1},{1,0},{2,3},{3,2},{4,5},{5,4},{6,7},{7,6},{8,9},{9,8},{10,11... | collective-permute-start | bytes 1572872 | tf_op jit(solution)/shard_map/ppermute | solution.py:108
  53.2 2.1 %collective-permute-done.14 = f16[256,512]{1,0:T(8,128)(2,1)S(1)} collective-permute-done((f16[256,512]{1,0:T(8,128)(2,1)S(1)}, f16[256,512]{1,0:T(8,128)(2,1)S(1)}, u32[]{:S(2)}, u32[]{:S(2)}) %collective-permute-start.14) | collective-permute-done | bytes 262176 | tf_op jit(solution)/shard_map/ppermute | solution.py:108
  58.8 7.7 %collective-permute-done.13 = f16[256,1024]{1,0:T(8,128)(2,1)S(1)} collective-permute-done((f16[256,1024]{1,0:T(8,128)(2,1)S(1)}, f16[256,1024]{1,0:T(8,128)(2,1)S(1)}, u32[]{:S(2)}, u32[]{:S(2)}) %collective-permute-start.13) | collective-permute-done | bytes 524320 | tf_op jit(solution)/shard_map/ppermute | solution.py:108
  68.8 9.0 %collective-permute-done.12 = f16[256,1024]{1,0:T(8,128)(2,1)S(1)} collective-permute-done((f16[256,1024]{1,0:T(8,128)(2,1)S(1)}, f16[256,1024]{1,0:T(8,128)(2,1)S(1)}, u32[]{:S(2)}, u32[]{:S(2)}) %collective-permute-start.12) | collective-permute-done | bytes 524320 | tf_op jit(solution)/shard_map/ppermute | solution.py:108
  80.2 8.8 %collective-permute-done.11 = f16[256,1024]{1,0:T(8,128)(2,1)S(1)} collective-permute-done((f16[256,1024]{1,0:T(8,128)(2,1)S(1)}, f16[256,1024]{1,0:T(8,128)(2,1)S(1)}, u32[]{:S(2)}, u32[]{:S(2)}) %collective-permute-start.11) | collective-permute-done | bytes 524320 | tf_op jit(solution)/shard_map/ppermute | solution.py:108
  89.3 8.2 %collective-permute-done.10 = f16[256,768]{1,0:T(8,128)(2,1)S(1)} collective-permute-done((f16[256,768]{1,0:T(8,128)(2,1)S(1)}, f16[256,768]{1,0:T(8,128)(2,1)S(1)}, u32[]{:S(2)}, u32[]{:S(2)}) %collective-permute-start.10) | collective-permute-done | bytes 393248 | tf_op jit(solution)/shard_map/ppermute | solution.py:108
  97.6 2.1 %shard_map.107 = (f32[8,256]{1,0:T(8,128)S(1)}, f32[1792,256]{1,0:T(8,128)S(1)}) custom-call(f32[256,1024]{1,0:T(8,128)S(1)} %get-tuple-element.111.logits_ref, s32[256,1]{1,0:T(8,128)S(1)} %get-tuple-element.57.target_ref, bf16[896,5120]{1,0:T(8,128)(2,1)S(1)} %shard_map.94.upper_ref, ...), custom_call_target="tpu_custom_call", output_to_operand_aliasing={{1}: (5, {})} | custom-call | flops 939524096 | bytes 8388608 | tf_op jit(solution)/shard_map/pallas_call | solution.py:189
  99.7 2.1 %shard_map.108 = (f32[8,256]{1,0:T(8,128)S(1)}, f32[1792,256]{1,0:T(8,128)S(1)}) custom-call(f32[256,1024]{1,0:T(8,128)S(1)} %get-tuple-element.109.logits_ref, s32[256,1]{1,0:T(8,128)S(1)} %get-tuple-element.57.target_ref, bf16[896,5120]{1,0:T(8,128)(2,1)S(1)} %shard_map.94.upper_ref, ...), custom_call_target="tpu_custom_call", output_to_operand_aliasing={{1}: (5, {})} | custom-call | flops 939524096 | bytes 8388608 | tf_op jit(solution)/shard_map/pallas_call | solution.py:189
  101.9 2.1 %shard_map.109 = (f32[8,256]{1,0:T(8,128)S(1)}, f32[1792,256]{1,0:T(8,128)S(1)}) custom-call(f32[256,1024]{1,0:T(8,128)S(1)} %get-tuple-element.107.logits_ref, s32[256,1]{1,0:T(8,128)S(1)} %get-tuple-element.57.target_ref, bf16[896,5120]{1,0:T(8,128)(2,1)S(1)} %shard_map.94.upper_ref, ...), custom_call_target="tpu_custom_call", output_to_operand_aliasing={{1}: (5, {})} | custom-call | flops 939524096 | bytes 8388608 | tf_op jit(solution)/shard_map/pallas_call | solution.py:189
  112.1 5.7 %collective-permute-done.22.got_ref = bf16[448,256]{1,0:T(8,128)(2,1)S(1)} collective-permute-done((bf16[448,256]{1,0:T(8,128)(2,1)S(1)}, bf16[448,256]{1,0:T(8,128)(2,1)S(1)}, u32[]{:S(2)}, u32[]{:S(2)}) %collective-permute-start.22) | collective-permute-done | bytes 229408 | tf_op jit(solution)/shard_map/ppermute | solution.py:104
  118.5 3.9 %collective-permute-done.17.got_ref = bf16[464,256]{1,0:T(8,128)(2,1)S(1)} collective-permute-done((bf16[464,256]{1,0:T(8,128)(2,1)S(1)}, bf16[464,256]{1,0:T(8,128)(2,1)S(1)}, u32[]{:S(2)}, u32[]{:S(2)}) %collective-permute-start.17) | collective-permute-done | bytes 237600 | tf_op jit(solution)/shard_map/ppermute | solution.py:104
  123.2 2.1 %collective-permute-start.19 = (bf16[256,128]{1,0:T(8,128)(2,1)S(1)}, bf16[256,128]{1,0:T(8,128)(2,1)S(1)}, u32[]{:S(2)}, u32[]{:S(2)}) collective-permute-start(bf16[256,128]{1,0:T(8,128)(2,1)S(1)} %get-tuple-element.81), channel_id=1, source_target_pairs={{0,16},{2,18},{4,20},{6,22},{8,24},{10,26},{12,28},{14,30},{16,0},... | collective-permute-start | bytes 196616 | tf_op jit(solution)/shard_map/ppermute | solution.py:104
  125.3 2.3 %collective-permute-start.20 = (bf16[256,128]{1,0:T(8,128)(2,1)S(1)}, bf16[256,128]{1,0:T(8,128)(2,1)S(1)}, u32[]{:S(2)}, u32[]{:S(2)}) collective-permute-start(bf16[256,128]{1,0:T(8,128)(2,1)S(1)} %get-tuple-element.82), channel_id=1, source_target_pairs={{0,24},{2,26},{4,28},{6,30},{8,16},{10,18},{12,20},{14,22},{16,8},... | collective-permute-start | bytes 196616 | tf_op jit(solution)/shard_map/ppermute | solution.py:104
  129.1 7.2 %collective-permute-done.24.picked_c_ref = bf16[224,128]{1,0:T(8,128)(2,1)S(1)} collective-permute-done((bf16[224,128]{1,0:T(8,128)(2,1)S(1)}, bf16[224,128]{1,0:T(8,128)(2,1)S(1)}, u32[]{:S(2)}, u32[]{:S(2)}) %collective-permute-start.24) | collective-permute-done | bytes 57376 | tf_op jit(solution)/shard_map/ppermute | solution.py:104
  137.9 4.4 %collective-permute-start.26 = (f32[16,128]{1,0:T(8,128)S(1)}, f32[16,128]{1,0:T(8,128)S(1)}, u32[]{:S(2)}, u32[]{:S(2)}) collective-permute-start(f32[16,128]{1,0:T(8,128)S(1)} %get-tuple-element.93.rows_ref), channel_id=1, source_target_pairs={{0,1},{1,0},{2,3},{3,2},{4,5},{5,4},{6,7},{7,6},{8,9},{9,8},{10,11... | collective-permute-start | bytes 24584 | tf_op jit(solution)/shard_map/ppermute | solution.py:108
  142.3 9.4 %shard_map.121 = bf16[1792,5120]{1,0:T(8,128)(2,1)} custom-call(bf16[1792,256]{1,0:T(8,128)(2,1)S(1)} %get-tuple-element.98.hidden_ref, f32[256,5120]{1,0:T(8,128)S(1)} %get-tuple-element.100.logits_ref, f32[256,8]{1,0:T(8,128)S(1)} %get-tuple-element.99.rows_ref, s32[256,1]{1,0:T(8,128)S(1)} %get-tuple-element.57.target_ref), custom_call_target="tpu_custom_call" | custom-call | flops 4697620480 | bytes 23592960 | tf_op jit(solution)/shard_map/pallas_call | solution.py:631
  (86 shorter events, 39.5 us)
Async XLA Ops:
  4.4 11.5 %collective-permute-start.1 = (bf16[224,128]{1,0:T(8,128)(2,1)S(1)}, bf16[224,128]{1,0:T(8,128)(2,1)S(1)}, u32[]{:S(2)}, u32[]{:S(2)}) collective-permute-start(bf16[224,128]{1,0:T(8,128)(2,1)S(1)} %broadcast_select_fusion), channel_id=1, source_target_pairs={{0,8},{2,10},{4,12},{6,14},{8,0},{10,2},{12,4},{14,6},{16,24},{18,... | collective-permute-start | bytes 172040 | tf_op jit(solution)/shard_map/ppermute | solution.py:104
  7.4 11.8 %collective-permute-start.2 = (bf16[224,128]{1,0:T(8,128)(2,1)S(1)}, bf16[224,128]{1,0:T(8,128)(2,1)S(1)}, u32[]{:S(2)}, u32[]{:S(2)}) collective-permute-start(bf16[224,128]{1,0:T(8,128)(2,1)S(1)} %broadcast_select_fusion), channel_id=1, source_target_pairs={{0,16},{2,18},{4,20},{6,22},{8,24},{10,26},{12,28},{14,30},{16,0},... | collective-permute-start | bytes 172040 | tf_op jit(solution)/shard_map/ppermute | solution.py:104
  21.8 9.8 %collective-permute-start.4 = (bf16[896,128]{1,0:T(8,128)(2,1)S(1)}, bf16[896,128]{1,0:T(8,128)(2,1)S(1)}, u32[]{:S(2)}, u32[]{:S(2)}) collective-permute-start(bf16[896,128]{1,0:T(8,128)(2,1)S(1)} %pad_maximum_fusion), channel_id=1, source_target_pairs={{0,4},{2,6},{4,0},{6,2},{8,12},{10,14},{12,8},{14,10},{16,20},{18,... | collective-permute-start | bytes 688136 | tf_op jit(solution)/shard_map/ppermute | solution.py:104
  23.4 7.5 %collective-permute-start.8 = (f32[8,128]{1,0:T(8,128)S(1)}, f32[8,128]{1,0:T(8,128)S(1)}, u32[]{:S(2)}, u32[]{:S(2)}) collective-permute-start(f32[8,128]{1,0:T(8,128)S(1)} %concatenate.9.own_ref), channel_id=1, source_target_pairs={{0,1},{1,0},{2,3},{3,2},{4,5},{5,4},{6,7},{7,6},{8,9},{9,8},{10,11... | collective-permute-start | bytes 12296 | tf_op jit(solution)/shard_map/ppermute | solution.py:108
  31.6 6.4 %collective-permute-start.5 = (bf16[896,128]{1,0:T(8,128)(2,1)S(1)}, bf16[896,128]{1,0:T(8,128)(2,1)S(1)}, u32[]{:S(2)}, u32[]{:S(2)}) collective-permute-start(bf16[896,128]{1,0:T(8,128)(2,1)S(1)} %pad_maximum_fusion), channel_id=1, source_target_pairs={{0,2},{2,0},{4,6},{6,4},{8,10},{10,8},{12,14},{14,12},{16,18},{18,... | collective-permute-start | bytes 688136 | tf_op jit(solution)/shard_map/ppermute | solution.py:104
  37.9 70.8 %collective-permute-start.21 = (bf16[896,256]{1,0:T(8,128)(2,1)S(1)}, bf16[896,256]{1,0:T(8,128)(2,1)S(1)}, u32[]{:S(2)}, u32[]{:S(2)}) collective-permute-start(bf16[896,256]{1,0:T(8,128)(2,1)S(1)} %get-tuple-element.85), channel_id=1, source_target_pairs={{0,2},{2,0},{4,6},{6,4},{8,10},{10,8},{12,14},{14,12},{16,18},{18,... | collective-permute-start | bytes 1376264 | tf_op jit(solution)/shard_map/ppermute | solution.py:104
  43.2 7.3 %collective-permute-start.15 = (f16[256,256]{1,0:T(8,128)(2,1)S(1)}, f16[256,256]{1,0:T(8,128)(2,1)S(1)}, u32[]{:S(2)}, u32[]{:S(2)}) collective-permute-start(f16[256,256]{1,0:T(8,128)(2,1)S(1)} %convert_element_type.78), channel_id=1, source_target_pairs={{0,1},{1,0},{2,3},{3,2},{4,5},{5,4},{6,7},{7,6},{8,9},{9,8},{10,11... | collective-permute-start | bytes 393224 | tf_op jit(solution)/shard_map/ppermute | solution.py:108
  46.1 9.2 %collective-permute-start.14 = (f16[256,512]{1,0:T(8,128)(2,1)S(1)}, f16[256,512]{1,0:T(8,128)(2,1)S(1)}, u32[]{:S(2)}, u32[]{:S(2)}) collective-permute-start(f16[256,512]{1,0:T(8,128)(2,1)S(1)} %convert_element_type.76), channel_id=1, source_target_pairs={{0,1},{1,0},{2,3},{3,2},{4,5},{5,4},{6,7},{7,6},{8,9},{9,8},{10,11... | collective-permute-start | bytes 786440 | tf_op jit(solution)/shard_map/ppermute | solution.py:108
  46.2 20.3 %collective-permute-start.13 = (f16[256,1024]{1,0:T(8,128)(2,1)S(1)}, f16[256,1024]{1,0:T(8,128)(2,1)S(1)}, u32[]{:S(2)}, u32[]{:S(2)}) collective-permute-start(f16[256,1024]{1,0:T(8,128)(2,1)S(1)} %convert_element_type.74), channel_id=1, source_target_pairs={{0,1},{1,0},{2,3},{3,2},{4,5},{5,4},{6,7},{7,6},{8,9},{9,8},{10,11... | collective-permute-start | bytes 1572872 | tf_op jit(solution)/shard_map/ppermute | solution.py:108
  48.4 29.4 %collective-permute-start.12 = (f16[256,1024]{1,0:T(8,128)(2,1)S(1)}, f16[256,1024]{1,0:T(8,128)(2,1)S(1)}, u32[]{:S(2)}, u32[]{:S(2)}) collective-permute-start(f16[256,1024]{1,0:T(8,128)(2,1)S(1)} %convert_element_type.72), channel_id=1, source_target_pairs={{0,1},{1,0},{2,3},{3,2},{4,5},{5,4},{6,7},{7,6},{8,9},{9,8},{10,11... | collective-permute-start | bytes 1572872 | tf_op jit(solution)/shard_map/ppermute | solution.py:108
  50.5 38.5 %collective-permute-start.11 = (f16[256,1024]{1,0:T(8,128)(2,1)S(1)}, f16[256,1024]{1,0:T(8,128)(2,1)S(1)}, u32[]{:S(2)}, u32[]{:S(2)}) collective-permute-start(f16[256,1024]{1,0:T(8,128)(2,1)S(1)} %convert_element_type.70), channel_id=1, source_target_pairs={{0,1},{1,0},{2,3},{3,2},{4,5},{5,4},{6,7},{7,6},{8,9},{9,8},{10,11... | collective-permute-start | bytes 1572872 | tf_op jit(solution)/shard_map/ppermute | solution.py:108
  55.3 42.1 %collective-permute-start.10 = (f16[256,768]{1,0:T(8,128)(2,1)S(1)}, f16[256,768]{1,0:T(8,128)(2,1)S(1)}, u32[]{:S(2)}, u32[]{:S(2)}) collective-permute-start(f16[256,768]{1,0:T(8,128)(2,1)S(1)} %convert_element_type.68), channel_id=1, source_target_pairs={{0,1},{1,0},{2,3},{3,2},{4,5},{5,4},{6,7},{7,6},{8,9},{9,8},{10,11... | collective-permute-start | bytes 1179656 | tf_op jit(solution)/shard_map/ppermute | solution.py:108
  66.6 35.3 %collective-permute-start.9 = (f16[256,256]{1,0:T(8,128)(2,1)S(1)}, f16[256,256]{1,0:T(8,128)(2,1)S(1)}, u32[]{:S(2)}, u32[]{:S(2)}) collective-permute-start(f16[256,256]{1,0:T(8,128)(2,1)S(1)} %convert_element_type.66), channel_id=1, source_target_pairs={{0,1},{1,0},{2,3},{3,2},{4,5},{5,4},{6,7},{7,6},{8,9},{9,8},{10,11... | collective-permute-start | bytes 393224 | tf_op jit(solution)/shard_map/ppermute | solution.py:108
  77.8 28.0 %collective-permute-start.7 = (f16[256,256]{1,0:T(8,128)(2,1)S(1)}, f16[256,256]{1,0:T(8,128)(2,1)S(1)}, u32[]{:S(2)}, u32[]{:S(2)}) collective-permute-start(f16[256,256]{1,0:T(8,128)(2,1)S(1)} %convert_element_type.64), channel_id=1, source_target_pairs={{0,1},{1,0},{2,3},{3,2},{4,5},{5,4},{6,7},{7,6},{8,9},{9,8},{10,11... | collective-permute-start | bytes 393224 | tf_op jit(solution)/shard_map/ppermute | solution.py:108
  109.2 8.5 %collective-permute-start.22 = (bf16[448,256]{1,0:T(8,128)(2,1)S(1)}, bf16[448,256]{1,0:T(8,128)(2,1)S(1)}, u32[]{:S(2)}, u32[]{:S(2)}) collective-permute-start(bf16[448,256]{1,0:T(8,128)(2,1)S(1)} %get-tuple-element.87), channel_id=1, source_target_pairs={{0,4},{2,6},{4,0},{6,2},{8,12},{10,14},{12,8},{14,10},{16,20},{18,... | collective-permute-start | bytes 688136 | tf_op jit(solution)/shard_map/ppermute | solution.py:104
  111.1 11.3 %collective-permute-start.17 = (bf16[464,256]{1,0:T(8,128)(2,1)S(1)}, bf16[464,256]{1,0:T(8,128)(2,1)S(1)}, u32[]{:S(2)}, u32[]{:S(2)}) collective-permute-start(bf16[464,256]{1,0:T(8,128)(2,1)S(1)} %get-tuple-element.77), channel_id=1, source_target_pairs={{0,4},{2,6},{4,0},{6,2},{8,12},{10,14},{12,8},{14,10},{16,20},{18,... | collective-permute-start | bytes 712712 | tf_op jit(solution)/shard_map/ppermute | solution.py:104
  118.5 9.1 %collective-permute-start.23 = (bf16[224,128]{1,0:T(8,128)(2,1)S(1)}, bf16[224,128]{1,0:T(8,128)(2,1)S(1)}, u32[]{:S(2)}, u32[]{:S(2)}) collective-permute-start(bf16[224,128]{1,0:T(8,128)(2,1)S(1)} %get-tuple-element.89), channel_id=1, source_target_pairs={{0,8},{2,10},{4,12},{6,14},{8,0},{10,2},{12,4},{14,6},{16,24},{18,... | collective-permute-start | bytes 172040 | tf_op jit(solution)/shard_map/ppermute | solution.py:104
  123.1 13.2 %collective-permute-start.18 = (bf16[256,128]{1,0:T(8,128)(2,1)S(1)}, bf16[256,128]{1,0:T(8,128)(2,1)S(1)}, u32[]{:S(2)}, u32[]{:S(2)}) collective-permute-start(bf16[256,128]{1,0:T(8,128)(2,1)S(1)} %get-tuple-element.80), channel_id=1, source_target_pairs={{0,8},{2,10},{4,12},{6,14},{8,0},{10,2},{12,4},{14,6},{16,24},{18,... | collective-permute-start | bytes 196616 | tf_op jit(solution)/shard_map/ppermute | solution.py:104
  123.2 13.1 %collective-permute-start.19 = (bf16[256,128]{1,0:T(8,128)(2,1)S(1)}, bf16[256,128]{1,0:T(8,128)(2,1)S(1)}, u32[]{:S(2)}, u32[]{:S(2)}) collective-permute-start(bf16[256,128]{1,0:T(8,128)(2,1)S(1)} %get-tuple-element.81), channel_id=1, source_target_pairs={{0,16},{2,18},{4,20},{6,22},{8,24},{10,26},{12,28},{14,30},{16,0},... | collective-permute-start | bytes 196616 | tf_op jit(solution)/shard_map/ppermute | solution.py:104
  125.3 11.0 %collective-permute-start.20 = (bf16[256,128]{1,0:T(8,128)(2,1)S(1)}, bf16[256,128]{1,0:T(8,128)(2,1)S(1)}, u32[]{:S(2)}, u32[]{:S(2)}) collective-permute-start(bf16[256,128]{1,0:T(8,128)(2,1)S(1)} %get-tuple-element.82), channel_id=1, source_target_pairs={{0,24},{2,26},{4,28},{6,30},{8,16},{10,18},{12,20},{14,22},{16,8},... | collective-permute-start | bytes 196616 | tf_op jit(solution)/shard_map/ppermute | solution.py:104
  127.6 8.7 %collective-permute-start.24 = (bf16[224,128]{1,0:T(8,128)(2,1)S(1)}, bf16[224,128]{1,0:T(8,128)(2,1)S(1)}, u32[]{:S(2)}, u32[]{:S(2)}) collective-permute-start(bf16[224,128]{1,0:T(8,128)(2,1)S(1)} %get-tuple-element.90), channel_id=1, source_target_pairs={{0,16},{2,18},{4,20},{6,22},{8,24},{10,26},{12,28},{14,30},{16,0},... | collective-permute-start | bytes 172040 | tf_op jit(solution)/shard_map/ppermute | solution.py:104
  127.6 8.7 %collective-permute-start.25 = (bf16[224,128]{1,0:T(8,128)(2,1)S(1)}, bf16[224,128]{1,0:T(8,128)(2,1)S(1)}, u32[]{:S(2)}, u32[]{:S(2)}) collective-permute-start(bf16[224,128]{1,0:T(8,128)(2,1)S(1)} %get-tuple-element.91), channel_id=1, source_target_pairs={{0,24},{2,26},{4,28},{6,30},{8,16},{10,18},{12,20},{14,22},{16,8},... | collective-permute-start | bytes 172040 | tf_op jit(solution)/shard_map/ppermute | solution.py:104
  137.2 14.5 %collective-permute-start.27 = (bf16[224,128]{1,0:T(8,128)(2,1)S(1)}, bf16[224,128]{1,0:T(8,128)(2,1)S(1)}, u32[]{:S(2)}, u32[]{:S(2)}) collective-permute-start(bf16[224,128]{1,0:T(8,128)(2,1)S(1)} %get-tuple-element.94.own_ref), channel_id=1, source_target_pairs={{16,1},{18,3},{20,5},{22,7},{24,9},{26,11},{28,13},{30,15},{1,16},... | collective-permute-start | bytes 172040 | tf_op jit(solution)/shard_map/ppermute | solution.py:118
  137.9 13.9 %collective-permute-start.26 = (f32[16,128]{1,0:T(8,128)S(1)}, f32[16,128]{1,0:T(8,128)S(1)}, u32[]{:S(2)}, u32[]{:S(2)}) collective-permute-start(f32[16,128]{1,0:T(8,128)S(1)} %get-tuple-element.93.rows_ref), channel_id=1, source_target_pairs={{0,1},{1,0},{2,3},{3,2},{4,5},{5,4},{6,7},{7,6},{8,9},{9,8},{10,11... | collective-permute-start | bytes 24584 | tf_op jit(solution)/shard_map/ppermute | solution.py:108
  (4 other events, 17.1 us)
